TPU v7x, 32 devices: a whole 2x2x4 slice. The times are simulated.
32 devices in a mesh: rows: 8 (over z, y), blk: 4 (over x, core).
Axes of the slice: x: 2, y: 2, z: 4, core: 2. Of those that a mesh axis runs over, the one named last changes fastest.
Arguments:
- tokens: bfloat16 [16, 512, 768], P('rows', 'blk'), may hold values from -6 to 6
- segment_ids: int32 [16, 512], P('rows'), may hold values from 0 to 8, as said below
- w_query: bfloat16 [768, 768], P(('rows', 'blk')), may hold values from -0.21875 to 0.21875
- w_key: bfloat16 [768, 768], P(('rows', 'blk')), may hold values from -0.21875 to 0.21875
- w_value: bfloat16 [768, 768], P(('rows', 'blk')), may hold values from -0.21875 to 0.21875
- w_output: bfloat16 [768, 768], P(('rows', 'blk')), may hold values from -0.875 to 0.875
- b_query: bfloat16 [768], P(('rows', 'blk')), may hold values from -3 to 3
- b_value: bfloat16 [768], P(('rows', 'blk')), may hold values from -3 to 3
- b_output: bfloat16 [768], P(('rows', 'blk')), may hold values from -3 to 3
- first_gain: bfloat16 [768], P(('rows', 'blk')), may hold values from 0.099609375 to 1.8984375
- first_shift: bfloat16 [768], P(('rows', 'blk')), may hold values from -3 to 3
- w_inner: bfloat16 [768, 3072], P(('rows', 'blk')), may hold values from -0.21875 to 0.21875
- b_inner: bfloat16 [3072], P(('rows', 'blk')), may hold values from -3 to 3
- w_outer: bfloat16 [3072, 768], P(('rows', 'blk')), may hold values from -0.109375 to 0.109375
- b_outer: bfloat16 [768], P(('rows', 'blk')), may hold values from -3 to 3
- second_gain: bfloat16 [768], P(('rows', 'blk')), may hold values from 0.099609375 to 1.8984375
- second_shift: bfloat16 [768], P(('rows', 'blk')), may hold values from -3 to 3
- cotangent: bfloat16 [16, 512, 768], P('rows', 'blk'), may hold values from -6 to 6
Outputs:
- block_out: bfloat16 [16, 512, 768], P('rows', 'blk')
- grad_tokens: float32 [16, 512, 768], P('rows', 'blk')
- grad_w_query: float32 [768, 768], P(('rows', 'blk'))
- grad_w_key: float32 [768, 768], P(('rows', 'blk'))
- grad_w_value: float32 [768, 768], P(('rows', 'blk'))
- grad_w_output: float32 [768, 768], P(('rows', 'blk'))
- grad_b_query: float32 [768], P(('rows', 'blk'))
- grad_b_value: float32 [768], P(('rows', 'blk'))
- grad_b_output: float32 [768], P(('rows', 'blk'))
- grad_first_gain: float32 [768], P(('rows', 'blk'))
- grad_first_shift: float32 [768], P(('rows', 'blk'))
- grad_w_inner: float32 [768, 3072], P(('rows', 'blk'))
- grad_b_inner: float32 [3072], P(('rows', 'blk'))
- grad_w_outer: float32 [3072, 768], P(('rows', 'blk'))
- grad_b_outer: float32 [768], P(('rows', 'blk'))
- grad_second_gain: float32 [768], P(('rows', 'blk'))
- grad_second_shift: float32 [768], P(('rows', 'blk'))
- rms_tokens: float32 [], replicated
- rms_attention: float32 [], replicated
Inputs may be any that keep to these rules, and one draw needn't show every extreme that they name: `segment_ids`: in each row the ids of the non-padding tokens never fall and run from 1 up to 8 (ids may be skipped, the last non-padding token has id 8); then padding (id 0) fills the row's tail, which every row has.
All inputs are finite; a program needn't handle non-finite values.
Results may differ from a plain program's by a relative error of at most 0.014.
Values may be sent and summed in bfloat16 or wider, within the bound.
A program may use at most 128 MiB of HBM per device.

v0:
```python
import jax
import jax.numpy as jnp
from jax import lax
from jax.sharding import PartitionSpec as P

HEADS = 12
HD = 64


EPSILON = 1e-06
MASKED = -1e30


def layer_norm(values, gain, shift):
    centre = values - jnp.mean(values, axis=-1, keepdims=True)
    spread = jnp.mean(centre * centre, axis=-1, keepdims=True)
    return centre * lax.rsqrt(spread + EPSILON) * gain + shift


def gelu_exact(values):
    return jax.nn.gelu(values, approximate=False)


def plain_product(left, right):
    return jnp.dot(left, right, preferred_element_type=jnp.float32)


def left_transpose(left, right):
    return lax.dot_general(
        left, right, (((0,), (0,)), ((), ())), preferred_element_type=jnp.float32
    )


def right_transpose(left, right):
    return lax.dot_general(
        left, right, (((1,), (1,)), ((), ())), preferred_element_type=jnp.float32
    )


def split_heads(rows_in):
    return rows_in.reshape(rows_in.shape[0], HEADS, HD)


def row_logits(query_heads, key_heads, query_ids, key_ids):
    scores = jnp.einsum("qhd,khd->hqk", query_heads, key_heads, preferred_element_type=jnp.float32)
    scores = scores * HD ** (-0.5)
    same = query_ids[:, None] == key_ids[None, :]
    return jnp.where(same[None], scores, MASKED)


def attend_row(pieces):
    query_row, key_row, value_row, query_ids, key_ids = pieces
    logits = row_logits(split_heads(query_row), split_heads(key_row), query_ids, key_ids)
    highest = jnp.max(logits, axis=-1, keepdims=True)
    raised = jnp.exp(logits - highest)
    totals = jnp.sum(raised, axis=-1, keepdims=True)
    probs_low = (raised / totals).astype(jnp.bfloat16)
    attended = jnp.einsum(
        "hqk,khd->qhd", probs_low, split_heads(value_row), preferred_element_type=jnp.float32
    )
    return (
        attended.reshape(query_row.shape[0], -1).astype(jnp.bfloat16),
        (highest + jnp.log(totals))[..., 0],
    )


def attend_back(pieces):
    query_row, key_row, value_row, query_ids, key_ids, log_totals, grad_row = pieces
    query_heads = split_heads(query_row)
    key_heads = split_heads(key_row)
    value_heads = split_heads(value_row)
    grad_heads = split_heads(grad_row)
    logits = row_logits(query_heads, key_heads, query_ids, key_ids)
    probs = jnp.exp(logits - log_totals[..., None])
    probs_low = probs.astype(jnp.bfloat16)
    grad_probs = jnp.einsum(
        "qhd,khd->hqk", grad_heads, value_heads, preferred_element_type=jnp.float32
    )
    weighted = jnp.sum(probs * grad_probs, axis=-1, keepdims=True)
    grad_scores = (probs * (grad_probs - weighted)).astype(jnp.bfloat16)
    scale = HD ** (-0.5)
    grad_query = (
        jnp.einsum("hqk,khd->qhd", grad_scores, key_heads, preferred_element_type=jnp.float32)
        * scale
    )
    grad_key = (
        jnp.einsum("hqk,qhd->khd", grad_scores, query_heads, preferred_element_type=jnp.float32)
        * scale
    )
    grad_value = jnp.einsum(
        "hqk,qhd->khd", probs_low, grad_heads, preferred_element_type=jnp.float32
    )
    return (
        grad_query.reshape(query_row.shape[0], -1).astype(jnp.bfloat16),
        grad_key.reshape(key_row.shape[0], -1),
        grad_value.reshape(key_row.shape[0], -1),
    )


def local(
    tokens,
    segment_ids,
    w_query,
    w_key,
    w_value,
    w_output,
    b_query,
    b_value,
    b_output,
    first_gain,
    first_shift,
    w_inner,
    b_inner,
    w_outer,
    b_outer,
    second_gain,
    second_shift,
    cotangent,
):
    rows_local, block_size, width = tokens.shape
    start = lax.axis_index("blk") * block_size
    query_ids = lax.dynamic_slice_in_dim(segment_ids, start, block_size, 1)
    valid = (query_ids > 0).astype(jnp.float32).reshape(-1, 1)
    (
        full_query,
        full_key,
        full_value,
        full_output,
        bias_query,
        bias_value,
        bias_output,
        gain_one,
        shift_one,
    ) = (
        lax.all_gather(w_query, ("rows", "blk"), axis=0, tiled=True),
        lax.all_gather(w_key, ("rows", "blk"), axis=0, tiled=True),
        lax.all_gather(w_value, ("rows", "blk"), axis=0, tiled=True),
        lax.all_gather(w_output, ("rows", "blk"), axis=0, tiled=True),
        lax.all_gather(b_query, ("rows", "blk"), axis=0, tiled=True),
        lax.all_gather(b_value, ("rows", "blk"), axis=0, tiled=True),
        lax.all_gather(b_output, ("rows", "blk"), axis=0, tiled=True),
        lax.all_gather(first_gain, ("rows", "blk"), axis=0, tiled=True),
        lax.all_gather(first_shift, ("rows", "blk"), axis=0, tiled=True),
    )
    flat = tokens.reshape(-1, width)
    keys = plain_product(flat, full_key).astype(jnp.bfloat16)
    values = (plain_product(flat, full_value) + bias_value).astype(jnp.bfloat16)
    keys_whole, values_whole = (
        lax.all_gather(keys.reshape(rows_local, block_size, width), "blk", axis=1, tiled=True),
        lax.all_gather(values.reshape(rows_local, block_size, width), "blk", axis=1, tiled=True),
    )
    queries = (plain_product(flat, full_query) + bias_query).astype(jnp.bfloat16)
    queries = queries.reshape(rows_local, block_size, width)
    full_inner, bias_inner, full_outer, bias_outer, gain_two, shift_two = (
        lax.all_gather(w_inner, ("rows", "blk"), axis=0, tiled=True),
        lax.all_gather(b_inner, ("rows", "blk"), axis=0, tiled=True),
        lax.all_gather(w_outer, ("rows", "blk"), axis=0, tiled=True),
        lax.all_gather(b_outer, ("rows", "blk"), axis=0, tiled=True),
        lax.all_gather(second_gain, ("rows", "blk"), axis=0, tiled=True),
        lax.all_gather(second_shift, ("rows", "blk"), axis=0, tiled=True),
    )
    attended, log_totals = lax.map(
        attend_row, (queries, keys_whole, values_whole, query_ids, segment_ids)
    )
    attended_flat = attended.reshape(-1, width)
    branch = plain_product(attended_flat, full_output) + bias_output
    flat_wide = flat.astype(jnp.float32)
    stat_sums = lax.psum(
        (jnp.sum(valid * flat_wide * flat_wide), jnp.sum(valid * branch * branch), jnp.sum(valid)),
        ("rows", "blk"),
    )
    first, first_back = jax.vjp(
        layer_norm, flat_wide + branch, gain_one.astype(jnp.float32), shift_one.astype(jnp.float32)
    )
    first_low = first.astype(jnp.bfloat16)
    inner = plain_product(first_low, full_inner) + bias_inner
    active_wide, gelu_back = jax.vjp(gelu_exact, inner)
    active = active_wide.astype(jnp.bfloat16)
    outer = plain_product(active, full_outer) + bias_outer
    result, second_back = jax.vjp(
        layer_norm, first + outer, gain_two.astype(jnp.float32), shift_two.astype(jnp.float32)
    )
    block_out = result.astype(jnp.bfloat16).reshape(tokens.shape)
    upstream = cotangent.reshape(-1, width).astype(jnp.float32) * valid
    grad_second, grad_gain_two, grad_shift_two = second_back(upstream)
    back_inner, back_outer = (
        lax.all_gather(w_inner, ("rows", "blk"), axis=0, tiled=True),
        lax.all_gather(w_outer, ("rows", "blk"), axis=0, tiled=True),
    )
    grad_outer = grad_second.astype(jnp.bfloat16)
    grad_bias_outer = jnp.sum(grad_outer.astype(jnp.float32), axis=0)
    grad_weight_outer = left_transpose(active, grad_outer)
    grad_active = right_transpose(grad_outer, back_outer)
    grad_inner = gelu_back(grad_active)[0].astype(jnp.bfloat16)
    grad_bias_inner = jnp.sum(grad_inner.astype(jnp.float32), axis=0)
    grad_weight_inner = left_transpose(first_low, grad_inner)
    ffn_shares = None
    grad_first = grad_second + right_transpose(grad_inner, back_inner)
    grad_resid, grad_gain_one, grad_shift_one = first_back(grad_first)
    back_query, back_key, back_value, back_output = (
        lax.all_gather(w_query, ("rows", "blk"), axis=0, tiled=True),
        lax.all_gather(w_key, ("rows", "blk"), axis=0, tiled=True),
        lax.all_gather(w_value, ("rows", "blk"), axis=0, tiled=True),
        lax.all_gather(w_output, ("rows", "blk"), axis=0, tiled=True),
    )
    grad_branch = grad_resid.astype(jnp.bfloat16)
    grad_bias_output = jnp.sum(grad_branch.astype(jnp.float32), axis=0)
    grad_weight_output = left_transpose(attended_flat, grad_branch)
    grad_attended = right_transpose(grad_branch, back_output).astype(jnp.bfloat16)
    grad_attended = grad_attended.reshape(rows_local, block_size, width)
    grad_queries, key_terms, value_terms = lax.map(
        attend_back,
        (queries, keys_whole, values_whole, query_ids, segment_ids, log_totals, grad_attended),
    )
    key_sums, value_sums = (
        lax.psum_scatter(
            key_terms.astype(jnp.bfloat16), "blk", scatter_dimension=1, tiled=True
        ).astype(jnp.float32),
        lax.psum_scatter(
            value_terms.astype(jnp.bfloat16), "blk", scatter_dimension=1, tiled=True
        ).astype(jnp.float32),
    )
    grad_query_flat = grad_queries.reshape(-1, width)
    grad_key_flat = key_sums.astype(jnp.bfloat16).reshape(-1, width)
    grad_value_flat = value_sums.astype(jnp.bfloat16).reshape(-1, width)
    grad_tokens = (
        grad_resid
        + right_transpose(grad_query_flat, back_query)
        + right_transpose(grad_key_flat, back_key)
        + right_transpose(grad_value_flat, back_value)
    )
    grad_weight_query = left_transpose(flat, grad_query_flat)
    grad_weight_key = left_transpose(flat, grad_key_flat)
    grad_weight_value = left_transpose(flat, grad_value_flat)
    grad_bias_query = jnp.sum(grad_query_flat.astype(jnp.float32), axis=0)
    grad_bias_value = jnp.sum(grad_value_flat.astype(jnp.float32), axis=0)
    everything = (
        lax.psum_scatter(grad_weight_query, ("rows", "blk"), scatter_dimension=0, tiled=True),
        lax.psum_scatter(grad_weight_key, ("rows", "blk"), scatter_dimension=0, tiled=True),
        lax.psum_scatter(grad_weight_value, ("rows", "blk"), scatter_dimension=0, tiled=True),
        lax.psum_scatter(grad_weight_output, ("rows", "blk"), scatter_dimension=0, tiled=True),
        lax.psum_scatter(grad_bias_query, ("rows", "blk"), scatter_dimension=0, tiled=True),
        lax.psum_scatter(grad_bias_value, ("rows", "blk"), scatter_dimension=0, tiled=True),
        lax.psum_scatter(grad_bias_output, ("rows", "blk"), scatter_dimension=0, tiled=True),
        lax.psum_scatter(grad_gain_one, ("rows", "blk"), scatter_dimension=0, tiled=True),
        lax.psum_scatter(grad_shift_one, ("rows", "blk"), scatter_dimension=0, tiled=True),
        lax.psum_scatter(grad_weight_inner, ("rows", "blk"), scatter_dimension=0, tiled=True),
        lax.psum_scatter(grad_bias_inner, ("rows", "blk"), scatter_dimension=0, tiled=True),
        lax.psum_scatter(grad_weight_outer, ("rows", "blk"), scatter_dimension=0, tiled=True),
        lax.psum_scatter(grad_bias_outer, ("rows", "blk"), scatter_dimension=0, tiled=True),
        lax.psum_scatter(grad_gain_two, ("rows", "blk"), scatter_dimension=0, tiled=True),
        lax.psum_scatter(grad_shift_two, ("rows", "blk"), scatter_dimension=0, tiled=True),
    )
    attn_shares = everything[:9]
    ffn_shares = everything[9:]
    rms_tokens = jnp.sqrt(stat_sums[0] / (stat_sums[2] * width))
    rms_attention = jnp.sqrt(stat_sums[1] / (stat_sums[2] * width))
    return (
        block_out,
        grad_tokens.reshape(tokens.shape),
        attn_shares[0],
        attn_shares[1],
        attn_shares[2],
        attn_shares[3],
        attn_shares[4],
        attn_shares[5],
        attn_shares[6],
        attn_shares[7],
        attn_shares[8],
        ffn_shares[0],
        ffn_shares[1],
        ffn_shares[2],
        ffn_shares[3],
        ffn_shares[4],
        ffn_shares[5],
        rms_tokens,
        rms_attention,
    )


def solution(mesh):
    placed = (
        P("rows", "blk", None),
        P("rows", None),
        P(("rows", "blk"), None),
        P(("rows", "blk"), None),
        P(("rows", "blk"), None),
        P(("rows", "blk"), None),
        P(("rows", "blk")),
        P(("rows", "blk")),
        P(("rows", "blk")),
        P(("rows", "blk")),
        P(("rows", "blk")),
        P(("rows", "blk"), None),
        P(("rows", "blk")),
        P(("rows", "blk"), None),
        P(("rows", "blk")),
        P(("rows", "blk")),
        P(("rows", "blk")),
        P("rows", "blk", None),
    )
    return jax.shard_map(
        local,
        mesh=mesh,
        in_specs=placed,
        out_specs=(
            P("rows", "blk", None),
            P("rows", "blk", None),
            P(("rows", "blk"), None),
            P(("rows", "blk"), None),
            P(("rows", "blk"), None),
            P(("rows", "blk"), None),
            P(("rows", "blk")),
            P(("rows", "blk")),
            P(("rows", "blk")),
            P(("rows", "blk")),
            P(("rows", "blk")),
            P(("rows", "blk"), None),
            P(("rows", "blk")),
            P(("rows", "blk"), None),
            P(("rows", "blk")),
            P(("rows", "blk")),
            P(("rows", "blk")),
            P(),
            P(),
        ),
        check_vma=False,
    )
```

profile of v0, /device:TPU:0, one launch (start us, length us, event | category | flops | bytes accessed | tf_op | source)
XLA Modules:
  0.0 1232.7 jit_solution(551471495514726393)
XLA Ops:
  17.0 42.5 %all-reduce.19 = (bf16[3072]{0:T(1024)(128)(2,1)S(1)}, bf16[768]{0:T(1024)(128)(2,1)S(1)}, bf16[768]{0:T(1024)(128)(2,1)S(1)}, bf16[768]{0:T(1024)(128)(2,1)S(1)...) all-reduce(bf16[3072]{0:T(1024)(128)(2,1)S(1)} %dynamic-update-slic, ...), channel_id=1, replica_groups=mesh['rows'=8,'blk'=4] {'rows','blk'}, use_global_device_ids=true, to_apply=%add.5 | all-reduce | flops 9216 | bytes 36864
  59.6 8.3 all-gather.9.cloned.1.call-done
  67.8 1.9 fusion.18
  70.7 52.8 %all-gather.15.cloned.1.call-done = bf16[768,768]{1,0:T(8,128)(2,1)} async-done(((bf16[24,768]{1,0:T(8,128)(2,1)}), bf16[768,768]{1,0:T(8,128)(2,1)}) %all-gather.15.cloned.1.call-update) | async-done | bytes 1179664 | tf_op jit(solution)/shard_map/all_gather | solution.py:136
  123.5 1.7 convolution_convert_fusion.1
  132.8 46.4 %all-gather.13.cloned.1.call-done = bf16[768,768]{1,0:T(8,128)(2,1)} async-done(((bf16[24,768]{1,0:T(8,128)(2,1)}), bf16[768,768]{1,0:T(8,128)(2,1)}) %all-gather.13.cloned.1.call-update) | async-done | bytes 1179664 | tf_op jit(solution)/shard_map/all_gather | solution.py:135
  179.3 1.7 fusion.19
  181.9 18.0 %all-gather.11.cloned.1.call-done = bf16[2,512,768]{1,2,0:T(8,128)(2,1)} async-done(((bf16[2,128,768]{1,2,0:T(8,128)(2,1)}), bf16[2,512,768]{1,2,0:T(8,128)(2,1)}) %all-gather.11.cloned.1.call-update) | async-done | bytes 1572880 | tf_op jit(solution)/shard_map/all_gather | solution.py:150
  200.0 21.8 %all-gather.17.cloned.1.call-done = bf16[2,512,768]{1,2,0:T(8,128)(2,1)} async-done(((bf16[2,128,768]{1,2,0:T(8,128)(2,1)}), bf16[2,512,768]{1,2,0:T(8,128)(2,1)}) %all-gather.17.cloned.1.call-update) | async-done | bytes 1572880 | tf_op jit(solution)/shard_map/all_gather | solution.py:149
  221.8 14.1 %while.26 = (s32[]{:T(128)}, bf16[2,128,768]{2,1,0:T(8,128)(2,1)S(1)}, f32[2,12,128]{2,1,0:T(8,128)}, bf16[2,512,768]{1,2,0:T(8,128)(2,1)}, s32[2,128]{1,0:T(2,1...) while((s32[]{:T(128)}, ...), condition=%wide.region_3.4_spmd, body=%wide.region_0.3_spmd.sunk | while | flops 210926080 | bytes 16050289 | solution.py:162
  222.6 1.5 constant_dynamic-slice_fusion.21
  229.7 1.5 constant_dynamic-slice_fusion.21
  235.9 42.6 %all-gather.19.cloned.1.call-done = bf16[768,768]{1,0:T(8,128)(2,1)} async-done(((bf16[24,768]{1,0:T(8,128)(2,1)}), bf16[768,768]{1,0:T(8,128)(2,1)}) %all-gather.19.cloned.1.call-update) | async-done | bytes 1179664 | tf_op jit(solution)/shard_map/all_gather | solution.py:138
  278.5 1.8 fusion.34
  280.7 63.3 %all-gather.21.cloned.1.call-done = bf16[768,3072]{1,0:T(8,128)(2,1)} async-done(((bf16[24,3072]{1,0:T(8,128)(2,1)}), bf16[768,3072]{1,0:T(8,128)(2,1)}) %all-gather.21.cloned.1.call-update) | async-done | bytes 4718608 | tf_op jit(solution)/shard_map/all_gather | solution.py:155
  344.0 11.3 multiply_convert_fusion.1
  355.3 53.5 %all-gather.23.cloned.1.call-done = bf16[3072,768]{1,0:T(8,128)(2,1)} async-done(((bf16[96,768]{1,0:T(8,128)(2,1)}), bf16[3072,768]{1,0:T(8,128)(2,1)}) %all-gather.23.cloned.1.call-update) | async-done | bytes 4718608 | tf_op jit(solution)/shard_map/all_gather | solution.py:157
  408.8 4.0 fusion.35
  415.8 2.7 convert_reduce_fusion
  418.6 2.2 multiply_reduce_fusion.3
  424.1 40.5 %while.27 = (s32[]{:T(128)}, bf16[2,128,768]{1,2,0:T(8,128)(2,1)}, bf16[2,512,768]{2,1,0:T(8,128)(2,1)}, bf16[2,512,768]{2,1,0:T(8,128)(2,1)}, bf16[2,512,768]{1...) while((s32[]{:T(128)}, bf16[2,128,768]{1,2,0:T(8,128)(2,1)}, ...), condition=%wide.region_14.15_spmd, body=%wide.region_12.14_spmd.sunk | while | flops 511441408 | bytes 61708604 | solution.py:211
  435.3 2.3 copy.115
  438.8 1.6 copy.114
  440.4 2.4 constant_dynamic-update-slice_fusion.9
  455.5 2.3 copy.115
  459.0 1.6 copy.114
  460.6 2.5 constant_dynamic-update-slice_fusion.9
  466.2 2.0 copy.75
  468.5 1.9 fusion.37
  470.5 20.6 %reduce-scatter.15.cloned.1.call-done = bf16[2,128,768]{2,1,0:T(8,128)(2,1)} async-done(((bf16[2,512,768]{2,1,0:T(8,128)(2,1)}), bf16[2,128,768]{2,1,0:T(8,128)(2,1)}) %reduce-scatter.15.cloned.1.call-update) | async-done | bytes 393232 | tf_op jit(solution)/shard_map/reduce_scatter | solution.py:216
  491.1 1.5 convolution_bitcast_fusion.1
  492.6 2.0 copy.77
  494.7 26.8 %reduce-scatter.17.cloned.1.call-done = bf16[2,128,768]{2,1,0:T(8,128)(2,1)} async-done(((bf16[2,512,768]{2,1,0:T(8,128)(2,1)}), bf16[2,128,768]{2,1,0:T(8,128)(2,1)}) %reduce-scatter.17.cloned.1.call-update) | async-done | bytes 393232 | tf_op jit(solution)/shard_map/reduce_scatter | solution.py:219
  521.6 1.5 convolution_bitcast_fusion
  523.1 2.0 copy.79
  526.5 5.9 fusion.28
  532.4 1.3 copy-done.22
  533.8 5.1 fusion.38
  539.9 1.6 fusion.20
  543.3 1.9 convolution_add_fusion.3
  545.3 41.4 %all-reduce.18 = (f32[768]{0:T(1024)S(1)}, f32[768]{0:T(1024)S(1)}, f32[768]{0:T(1024)S(1)}, f32[768]{0:T(1024)S(1)}, f32[768]{0:T(1024)S(1)}, /*index=5*/f32[30...) all-reduce(f32[768]{0:T(1024)} %convert_reduce_fusion.4, ...), channel_id=8, replica_groups=mesh['rows'=8,'blk'=4] {'rows','blk'}, use_global_device_ids=true, to_apply=%region_22.23.clone | all-reduce | flops 9219 | bytes 73752
  594.5 1.4 convolution_add_fusion.1
  595.8 31.5 %reduce-scatter.25.cloned.1.call-done = f32[24,768]{1,0:T(8,128)} async-done(((f32[768,768]{1,0:T(8,128)}), f32[24,768]{1,0:T(8,128)}) %reduce-scatter.25.cloned.1.call-update) | async-done | bytes 73744
  627.4 104.3 %reduce-scatter.19.cloned.1.call-done = f32[24,768]{1,0:T(8,128)} async-done(((f32[768,768]{1,0:T(8,128)}), f32[24,768]{1,0:T(8,128)}) %reduce-scatter.19.cloned.1.call-update) | async-done | bytes 73744 | tf_op jit(solution)/shard_map/reduce_scatter | solution.py:241
  731.7 104.6 %reduce-scatter.27.cloned.1.call-done = f32[24,768]{1,0:T(8,128)} async-done(((f32[768,768]{1,0:T(8,128)}), f32[24,768]{1,0:T(8,128)}) %reduce-scatter.27.cloned.1.call-update) | async-done | bytes 73744
  836.3 104.5 %reduce-scatter.29.cloned.1.call-done = f32[24,768]{1,0:T(8,128)} async-done(((f32[768,768]{1,0:T(8,128)}), f32[24,768]{1,0:T(8,128)}) %reduce-scatter.29.cloned.1.call-update) | async-done | bytes 73744
  940.8 141.7 %reduce-scatter.21.cloned.1.call-done = f32[24,3072]{1,0:T(8,128)} async-done(((f32[768,3072]{1,0:T(8,128)}), f32[24,3072]{1,0:T(8,128)}) %reduce-scatter.21.cloned.1.call-update) | async-done | bytes 294928 | tf_op jit(solution)/shard_map/reduce_scatter | solution.py:247
  1082.5 141.5 %reduce-scatter.23.cloned.1.call-done = f32[96,768]{1,0:T(8,128)} async-done(((f32[3072,768]{1,0:T(8,128)}), f32[96,768]{1,0:T(8,128)}) %reduce-scatter.23.cloned.1.call-update) | async-done | bytes 294928 | tf_op jit(solution)/shard_map/reduce_scatter | solution.py:249
  (258 shorter events, 76.1 us)
Async XLA Ops:
  7.2 116.3 %copy-start.4 = (bf16[2,128,768]{2,1,0:T(8,128)(2,1)S(1)}, bf16[2,128,768]{2,1,0:T(8,128)(2,1)}, u32[]{:S(2)}) copy-start(bf16[2,128,768]{2,1,0:T(8,128)(2,1)} %param.22) | copy-start | bytes 1179652
  7.2 60.6 %all-gather.9.cloned.1.call-start = ((), (), s32[]{:S(2)}) async-start(), calls=%async_computation.8 | async-start | bytes 1216512 | tf_op jit(solution)/shard_map/all_gather | solution.py:137
  7.9 115.6 %all-gather.15.cloned.1.call-start = ((), (), s32[]{:S(2)}) async-start(), calls=%async_computation.11 | async-start | bytes 1216512 | tf_op jit(solution)/shard_map/all_gather | solution.py:136
  8.7 170.6 %all-gather.13.cloned.1.call-start = ((), (), s32[]{:S(2)}) async-start(), calls=%async_computation.10 | async-start | bytes 1216512 | tf_op jit(solution)/shard_map/all_gather | solution.py:135
  9.4 190.6 %all-gather.11.cloned.1.call-start = ((), (), s32[]{:S(2)}) async-start(), calls=%async_computation.9 | async-start | bytes 1966080 | tf_op jit(solution)/shard_map/all_gather | solution.py:150
  67.8 62.6 %copy-start.31 = (s32[2,512]{1,0:T(2,128)S(1)}, s32[2,512]{1,0:T(2,128)}, u32[]{:S(2)}) copy-start(s32[2,512]{1,0:T(2,128)} %param.23) | copy-start | bytes 12292
  70.7 151.1 %all-gather.17.cloned.1.call-start = ((), (), s32[]{:S(2)}) async-start(), calls=%async_computation.12 | async-start | bytes 1966080 | tf_op jit(solution)/shard_map/all_gather | solution.py:149
  126.2 152.3 %all-gather.19.cloned.1.call-start = ((), (), s32[]{:S(2)}) async-start(), calls=%async_computation.13 | async-start | bytes 1216512 | tf_op jit(solution)/shard_map/all_gather | solution.py:138
  126.8 217.2 %all-gather.21.cloned.1.call-start = ((), (), s32[]{:S(2)}) async-start(), calls=%async_computation.14 | async-start | bytes 4866048 | tf_op jit(solution)/shard_map/all_gather | solution.py:155
  127.5 281.3 %all-gather.23.cloned.1.call-start = ((), (), s32[]{:S(2)}) async-start(), calls=%async_computation.15 | async-start | bytes 4866048 | tf_op jit(solution)/shard_map/all_gather | solution.py:157
  128.3 362.8 %reduce-scatter.15.cloned.1.call-start = ((), (), s32[]{:S(2)}) async-start(), calls=%async_computation.16 | async-start | bytes 1966080 | tf_op jit(solution)/shard_map/reduce_scatter | solution.py:216
  235.9 44.7 %copy-start.26 = (bf16[2,128,768]{2,1,0:T(8,128)(2,1)}, bf16[2,128,768]{2,1,0:T(8,128)(2,1)S(1)}, u32[]{:S(2)}) copy-start(bf16[2,128,768]{2,1,0:T(8,128)(2,1)S(1)} %get-tuple-element.121) | copy-start | bytes 1179652
  280.4 140.5 %copy-start.6 = (f32[256,768]{1,0:T(8,128)}, f32[256,768]{1,0:T(8,128)S(1)}, u32[]{:S(2)}) copy-start(f32[256,768]{1,0:T(8,128)S(1)} %get-tuple-element.322) | copy-start | bytes 2359300
  280.4 140.5 %copy-start.32 = (f32[256]{0:T(256)}, f32[256]{0:T(256)S(1)}, u32[]{:S(2)}) copy-start(f32[256]{0:T(256)S(1)} %broadcast_multiply_fusion.1) | copy-start | bytes 3076
  280.6 140.2 %copy-start.37 = (f32[256]{0:T(256)}, f32[256]{0:T(256)S(1)}, u32[]{:S(2)}) copy-start(f32[256]{0:T(256)S(1)} %fusion.24) | copy-start | bytes 3076
  280.6 128.2 %copy-start.40 = (f32[768]{0:T(1024)S(1)}, f32[768]{0:T(1024)}, u32[]{:S(2)}) copy-start(f32[768]{0:T(1024)} %convert_element_type.155) | copy-start | bytes 9220
  355.3 57.6 %copy-start.21 = (bf16[256,3072]{1,0:T(8,128)(2,1)}, bf16[256,3072]{1,0:T(8,128)(2,1)S(1)}, u32[]{:S(2)}) copy-start(bf16[256,3072]{1,0:T(8,128)(2,1)S(1)} %get-tuple-element.319) | copy-start | bytes 4718596
  408.8 6.7 slice-start.2
  408.8 4.3 copy-start.19
  408.8 4.3 copy-start.38
  408.8 5.4 copy-start.36
  408.8 6.7 slice-start.3
  412.8 3.0 copy-start.42
  415.4 3.2 slice-start
  415.5 3.0 copy-start.23
  415.8 2.8 slice-start.1
  429.0 3.2 copy-start.2
  438.8 4.0 copy-start.1
  438.8 4.0 copy-start.3
  440.4 3.1 copy-start.13
  449.2 3.2 copy-start.2
  459.0 4.1 copy-start.1
  459.0 4.1 copy-start.3
  460.6 3.2 copy-start.13
  464.6 57.0 %reduce-scatter.17.cloned.1.call-start = ((), (), s32[]{:S(2)}) async-start(), calls=%async_computation.17 | async-start | bytes 1966080 | tf_op jit(solution)/shard_map/reduce_scatter | solution.py:219
  465.2 162.2 %reduce-scatter.25.cloned.1.call-start = ((), (), s32[]{:S(2)}) async-start(), calls=%async_computation.21 | async-start | bytes 2433024
  468.2 263.6 %reduce-scatter.19.cloned.1.call-start = ((), (), s32[]{:S(2)}) async-start(), calls=%async_computation.18 | async-start | bytes 2433024 | tf_op jit(solution)/shard_map/reduce_scatter | solution.py:241
  470.5 365.8 %reduce-scatter.27.cloned.1.call-start = ((), (), s32[]{:S(2)}) async-start(), calls=%async_computation.22 | async-start | bytes 2433024
  494.7 446.1 %reduce-scatter.29.cloned.1.call-start = ((), (), s32[]{:S(2)}) async-start(), calls=%async_computation.23 | async-start | bytes 2433024
  525.1 557.4 %reduce-scatter.21.cloned.1.call-start = ((), (), s32[]{:S(2)}) async-start(), calls=%async_computation.19 | async-start | bytes 9732096 | tf_op jit(solution)/shard_map/reduce_scatter | solution.py:247
  532.4 691.6 %reduce-scatter.23.cloned.1.call-start = ((), (), s32[]{:S(2)}) async-start(), calls=%async_computation.20 | async-start | bytes 9732096 | tf_op jit(solution)/shard_map/reduce_scatter | solution.py:249
  538.9 4.4 copy-start.9
  539.0 6.2 copy-start.12
  539.0 6.3 copy-start.34
  539.0 6.3 copy-start.35
  539.0 55.0 %copy-start.10 = (bf16[768,768]{1,0:T(8,128)(2,1)S(1)}, bf16[768,768]{1,0:T(8,128)(2,1)}, u32[]{:S(2)}) copy-start(bf16[768,768]{1,0:T(8,128)(2,1)} %all-gather.15.cloned.1.call-done) | copy-start | bytes 3538948
  541.6 52.4 %copy-start.25 = (bf16[2,128,768]{2,1,0:T(8,128)(2,1)S(1)}, bf16[2,128,768]{2,1,0:T(8,128)(2,1)}, u32[]{:S(2)}) copy-start(bf16[2,128,768]{2,1,0:T(8,128)(2,1)} %reduce-scatter.15.cloned.1.call-done) | copy-start | bytes 1179652
  588.7 5.8 copy-start.30
  (21 other events, 33.4 us)
Sparse Core Ops, SparseCore 0:
  10.9 56.8 all-gather.8
  70.7 52.7 all-gather.14
  126.4 52.8 all-gather.12
  181.3 18.6 all-gather.10
  202.0 19.8 all-gather.16
  224.6 53.9 all-gather.18
  281.4 62.4 all-gather.20
  346.9 61.9 all-gather.22
  464.7 26.3 reduce-scatter.14
  493.5 28.0 reduce-scatter.16
  527.4 99.8 reduce-scatter.24
  633.1 98.5 reduce-scatter.18
  737.6 98.6 reduce-scatter.26
  842.0 98.6 reduce-scatter.28
  947.1 135.3 reduce-scatter.20
  1088.8 135.1 reduce-scatter.22
where the time goes:
time: 1230 us
  waiting for transfers between devices  987 us (80%)
  blocking collectives  83.9 us (7%)
  matrix products  63.3 us (5%)
  local copies, waits for them, and re-layouts  63 us (5%)
  between operations  18.9 us (2%)
  other arithmetic  15.3 us (1%)
    unnamed x19, waiting for transfers between devices  245 us
    reduce_scatter x1, waiting for transfers between devices, local(): lax.psum_scatter(grad_weight_inner, ('rows', 'blk'), scatter_dimension=0,...  142 us
    reduce_scatter x1, waiting for transfers between devices, local(): lax.psum_scatter(grad_weight_outer, ('rows', 'blk'), scatter_dimension=0,...  141 us
    reduce_scatter x1, waiting for transfers between devices, local(): lax.psum_scatter(grad_weight_output, ('rows', 'blk'), scatter_dimension=0...  104 us
    unnamed x2, blocking collectives  83.9 us
    all_gather x1, waiting for transfers between devices, local(): lax.all_gather(w_inner, ('rows', 'blk'), axis=0, tiled=True)  63.3 us
    all_gather x1, waiting for transfers between devices, local(): lax.all_gather(w_outer, ('rows', 'blk'), axis=0, tiled=True)  53.5 us
    all_gather x1, waiting for transfers between devices, local(): lax.all_gather(w_key, ('rows', 'blk'), axis=0, tiled=True)  52.8 us
  transfers between devices with their start and end apart: 16, of which 16 were waited for; matrix products, arithmetic and copies ran while one was open for 7% of the time, Pallas kernels for 0%

commit v1 on v0

v1 whole, which is shorter than its diff:
```python
import functools
import math

import jax
import jax.numpy as jnp
from jax import lax
from jax.experimental import pallas as pl
from jax.experimental.pallas import tpu as pltpu
from jax.sharding import PartitionSpec as P

HEADS = 12
HD = 64
EVERY = slice(None)
MESH = pl.DeviceIdType.MESH


class Grid:
    def __init__(self, rows, blk):
        if rows <= 8:
            self.size = {"z": rows // 2, "y": 2, "x": blk // 2, "c": 2}
            self.in_rows, self.in_blk = ("z", "y"), ("x", "c")
        else:
            self.size = {"z": rows // 8, "y": 4, "x": blk, "c": 2}
            self.in_rows, self.in_blk = ("z", "y", "c"), ("x",)
        self.order = self.in_rows + self.in_blk

    def dims(self, axes):
        return tuple(self.size[a] for a in axes)

    def here(self):
        place = {}
        for name, axes in (("rows", self.in_rows), ("blk", self.in_blk)):
            index = lax.axis_index(name)
            for a in reversed(axes):
                place[a] = lax.rem(index, self.size[a])
                index = index // self.size[a]
        return place

    def device(self, place):
        found = []
        for axes in (self.in_rows, self.in_blk):
            index = 0
            for a in axes:
                index = index * self.size[a] + place[a]
            found.append(index)
        return tuple(found)

    def toward(self, me, axis, step):
        return {**me, axis: lax.rem(me[axis] + step, self.size[axis])}

    def away(self, me, axis, step):
        return lax.rem(me[axis] + self.size[axis] - step, self.size[axis])

    def greet(self, me, axes):
        barrier = pltpu.get_barrier_semaphore()
        count = 0
        for a in axes:
            for k in range(1, self.size[a]):
                pl.semaphore_signal(
                    barrier, inc=1, device_id=self.device(self.toward(me, a, k)), device_id_type=MESH
                )
                count += 1
        pl.semaphore_wait(barrier, count)


def piece(ref, lead, cut):
    if cut is None:
        return ref.at[lead] if lead else ref
    dim, start, size = cut
    tail = (pl.ds(start, size), EVERY) if dim == 0 else (EVERY, pl.ds(start, size))
    return ref.at[(*lead, *tail)]


def cut_shape(shape, cut):
    if cut is None:
        return tuple(shape)
    dim, _, size = cut
    return (size, shape[1]) if dim == 0 else (shape[0], size)


def halves(rows, columns):
    if rows % 32 == 0:
        return (0, 0, rows // 2), (0, rows // 2, rows // 2)
    return (1, 0, columns // 2), (1, columns // 2, columns // 2)


def gather_body(grid, axes_of, chunks, ahead, lags, *refs):
    n = len(axes_of)
    ins, outs = refs[:n], refs[n : 2 * n]
    send_sem, recv_sem, core_send, core_recv, keep_sem = refs[2 * n :]
    me = grid.here()
    grid.greet(me, grid.order)
    sibling = grid.device(grid.toward(me, "c", 1))
    other = grid.toward(me, "c", 1)["c"]
    sent = []

    def lead(i, **over):
        return tuple(over.get(a, me[a]) for a in axes_of[i])

    kept = []
    for i in range(n):
        copy = pltpu.make_async_copy(ins[i], outs[i].at[lead(i)], keep_sem.at[i])
        copy.start()
        kept.append(copy)

    def ship(t, j, start):
        i, cut, phases = chunks[t]
        axis = phases[j]
        got = {a: EVERY for a in phases[:j]}
        mine = piece(outs[i], lead(i, **got), cut)
        source = piece(ins[i], (), cut) if j == 0 else mine
        for k in range(1, grid.size[axis]):
            sems = send_sem.at[t, j, k - 1], recv_sem.at[t, j, k - 1]
            if start:
                copy = pltpu.make_async_remote_copy(
                    source, mine, *sems,
                    device_id=grid.device(grid.toward(me, axis, k)), device_id_type=MESH,
                )
                copy.start()
                sent.append(copy)
            else:
                theirs = piece(outs[i], lead(i, **got, **{axis: grid.away(me, axis, k)}), cut)
                pltpu.make_async_remote_copy(
                    source, theirs, *sems, device_id=sibling, device_id_type=MESH
                ).wait_recv()

    def pass_on(t, j, start):
        i, cut, phases = chunks[t]
        if "c" not in axes_of[i]:
            return
        if j == 0:
            places = [{}]
        else:
            axis = phases[j - 1]
            got = {a: EVERY for a in phases[: j - 1]}
            places = [{**got, axis: grid.away(me, axis, k)} for k in range(1, grid.size[axis])]
        for p, place in enumerate(places):
            mine = piece(outs[i], lead(i, **place), cut)
            sems = core_send.at[t, j, p], core_recv.at[t, j, p]
            if start:
                source = piece(ins[i], (), cut) if j == 0 else mine
                copy = pltpu.make_async_remote_copy(
                    source, mine, *sems, device_id=sibling, device_id_type=MESH
                )
                copy.start()
                sent.append(copy)
            else:
                theirs = piece(outs[i], lead(i, **place, c=other), cut)
                pltpu.make_async_remote_copy(
                    mine, theirs, *sems, device_id=sibling, device_id_type=MESH
                ).wait_recv()

    count = len(chunks)

    def begin(t):
        ship(t, 0, True)
        pass_on(t, 0, True)

    for t in range(min(ahead, count)):
        begin(t)
    for copy in kept:
        copy.wait()
    stages = max(len(c[2]) for c in chunks)
    starts = [sum(lags[:j]) for j in range(stages)]
    for s in range(count + starts[-1]):
        if s + ahead < count:
            begin(s + ahead)
        for j in range(stages):
            t = s - starts[j]
            if 0 <= t < count and j < len(chunks[t][2]):
                ship(t, j, False)
                if j + 1 < len(chunks[t][2]):
                    ship(t, j + 1, True)
                pass_on(t, j + 1, True)
    for t in range(count):
        for j in range(len(chunks[t][2]) + 1):
            pass_on(t, j, False)
    for copy in sent:
        copy.wait_send()


def gather(grid, arrays, axes_of, chunks, ident, ahead=4, lags=(1, 3, 3)):
    count = len(chunks)
    widest = max(grid.size.values())
    stages = max(len(c[2]) for c in chunks)
    dma = pltpu.SemaphoreType.DMA
    return pl.pallas_call(
        functools.partial(gather_body, grid, axes_of, chunks, ahead, lags),
        out_shape=[
            jax.ShapeDtypeStruct((*grid.dims(axes), *a.shape), a.dtype)
            for a, axes in zip(arrays, axes_of)
        ],
        in_specs=[pl.BlockSpec(memory_space=pltpu.VMEM)] * len(arrays),
        out_specs=[pl.BlockSpec(memory_space=pl.ANY)] * len(arrays),
        scratch_shapes=[
            dma((count, stages, widest - 1)),
            dma((count, stages, widest - 1)),
            dma((count, stages + 1, widest - 1)),
            dma((count, stages + 1, widest - 1)),
            dma((len(arrays),)),
        ],
        compiler_params=pltpu.CompilerParams(collective_id=ident, has_side_effects=True),
        name="gather_" + str(ident),
    )(*arrays)


def scatter_body(grid, axes_of, chunks, lags, n, *refs):
    ins, outs = refs[:n], refs[n : 2 * n]
    send_sem, recv_sem, own_sem = refs[2 * n : 2 * n + 3]
    scratch = list(refs[2 * n + 3 :])
    own, landed = [], []
    for _, _, phases in chunks:
        own.append(scratch.pop(0))
        landed.append([scratch.pop(0) for _ in phases])
    me = grid.here()
    used = []
    for _, _, phases in chunks:
        used += [a for a in phases if a not in used]
    grid.greet(me, used)
    sent = []

    def source(t, j, place):
        i, cut, phases = chunks[t]
        axis = phases[j]
        rest = [a for a in axes_of[i] if a not in phases[:j]]
        lead = tuple(place if a == axis else EVERY for a in rest)
        if j == 0:
            return piece(ins[i], lead, cut)
        return landed[t][j - 1].at[(0, *lead)]

    def ship(t, j):
        axis = chunks[t][2][j]
        for k in range(1, grid.size[axis]):
            to = grid.toward(me, axis, k)
            copy = pltpu.make_async_remote_copy(
                source(t, j, to[axis]), landed[t][j].at[k - 1],
                send_sem.at[t, j, k - 1], recv_sem.at[t, j, k - 1],
                device_id=grid.device(to), device_id_type=MESH,
            )
            copy.start()
            sent.append(copy)

    def keep(t):
        i, cut, phases = chunks[t]
        return pltpu.make_async_copy(source(t, 0, me[phases[0]]), own[t], own_sem.at[t])

    def absorb(t, j):
        i, cut, phases = chunks[t]
        axis = phases[j]
        parts = grid.size[axis] - 1
        for k in range(parts):
            pltpu.make_async_remote_copy(
                landed[t][j].at[k], landed[t][j].at[k],
                send_sem.at[t, j, k], recv_sem.at[t, j, k],
                device_id=grid.device(grid.toward(me, axis, 1)), device_id_type=MESH,
            ).wait_recv()
        if j == 0:
            keep(t).wait()
        rest = [a for a in axes_of[i] if a not in phases[: j + 1]]
        before = [a for a in axes_of[i] if a not in phases[:j]]
        last = j == len(phases) - 1

        def add(f, carry):
            place, index = {axis: me[axis]}, f
            for a in reversed(rest):
                place[a] = lax.rem(index, grid.size[a])
                index = index // grid.size[a]
            spot = tuple(place[a] for a in rest)
            if j == 0:
                mine = own[t][spot]
            else:
                mine = landed[t][j - 1][(0, *(place[a] for a in before))]
            terms = [landed[t][j][(k, *spot)] for k in range(parts)]
            if last or parts > 1:
                total = mine.astype(jnp.float32)
                for term in terms:
                    total = total + term.astype(jnp.float32)
            else:
                total = mine + terms[0]
            if last:
                if cut is None:
                    outs[i][...] = total.astype(outs[i].dtype)
                else:
                    dim, begin, size = cut
                    if dim == 0:
                        outs[i][begin : begin + size, :] = total.astype(outs[i].dtype)
                    else:
                        outs[i][:, begin : begin + size] = total.astype(outs[i].dtype)
            else:
                landed[t][j][(0, *spot)] = total.astype(mine.dtype)
            return carry

        steps = math.prod(grid.dims(rest))
        if steps == 1:
            add(0, 0)
        else:
            lax.fori_loop(0, steps, add, 0)

    count = len(chunks)
    for t in range(count):
        ship(t, 0)
        keep(t).start()
    stages = max(len(c[2]) for c in chunks)
    starts = [sum(lags[:j]) for j in range(stages)]
    for s in range(count + starts[-1]):
        for j in range(stages):
            t = s - starts[j]
            if 0 <= t < count and j < len(chunks[t][2]):
                absorb(t, j)
                if j + 1 < len(chunks[t][2]):
                    ship(t, j + 1)
    for copy in sent:
        copy.wait_send()


def scatter(grid, arrays, axes_of, chunks, kinds, ident, lags=(1, 2, 2)):
    count = len(chunks)
    widest = max(grid.size.values())
    stages = max(len(c[2]) for c in chunks)
    dma = pltpu.SemaphoreType.DMA
    blocks = [a.shape[len(axes) :] for a, axes in zip(arrays, axes_of)]
    room = []
    for i, cut, phases in chunks:
        shape = cut_shape(blocks[i], cut)
        for j in range(len(phases)):
            rest = grid.dims([a for a in axes_of[i] if a not in phases[: j + 1]])
            if j == 0:
                room.append(pltpu.VMEM((*rest, *shape), arrays[i].dtype))
            room.append(pltpu.VMEM((grid.size[phases[j]] - 1, *rest, *shape), arrays[i].dtype))
    return pl.pallas_call(
        functools.partial(scatter_body, grid, axes_of, chunks, lags, len(arrays)),
        out_shape=[jax.ShapeDtypeStruct(b, k) for b, k in zip(blocks, kinds)],
        in_specs=[pl.BlockSpec(memory_space=pl.ANY)] * len(arrays),
        out_specs=[pl.BlockSpec(memory_space=pltpu.VMEM)] * len(arrays),
        scratch_shapes=[
            dma((count, stages, widest - 1)),
            dma((count, stages, widest - 1)),
            dma((count,)),
            *room,
        ],
        compiler_params=pltpu.CompilerParams(
            collective_id=ident, has_side_effects=True, vmem_limit_bytes=60 * 2**20
        ),
        name="scatter_" + str(ident),
    )(*arrays)


EPSILON = 1e-06
MASKED = -1e30


def layer_norm(values, gain, shift):
    centre = values - jnp.mean(values, axis=-1, keepdims=True)
    spread = jnp.mean(centre * centre, axis=-1, keepdims=True)
    return centre * lax.rsqrt(spread + EPSILON) * gain + shift


def gelu_exact(values):
    return jax.nn.gelu(values, approximate=False)


def plain_product(left, right):
    return jnp.dot(left, right, preferred_element_type=jnp.float32)


def left_transpose(left, right):
    return lax.dot_general(
        left, right, (((0,), (0,)), ((), ())), preferred_element_type=jnp.float32
    )


def right_transpose(left, right):
    return lax.dot_general(
        left, right, (((1,), (1,)), ((), ())), preferred_element_type=jnp.float32
    )


def split_heads(rows_in):
    return rows_in.reshape(rows_in.shape[0], HEADS, HD)


def row_logits(query_heads, key_heads, query_ids, key_ids):
    scores = jnp.einsum("qhd,khd->hqk", query_heads, key_heads, preferred_element_type=jnp.float32)
    scores = scores * HD ** (-0.5)
    same = query_ids[:, None] == key_ids[None, :]
    return jnp.where(same[None], scores, MASKED)


def attend_row(pieces):
    query_row, key_row, value_row, query_ids, key_ids = pieces
    logits = row_logits(split_heads(query_row), split_heads(key_row), query_ids, key_ids)
    highest = jnp.max(logits, axis=-1, keepdims=True)
    raised = jnp.exp(logits - highest)
    totals = jnp.sum(raised, axis=-1, keepdims=True)
    probs_low = (raised / totals).astype(jnp.bfloat16)
    attended = jnp.einsum(
        "hqk,khd->qhd", probs_low, split_heads(value_row), preferred_element_type=jnp.float32
    )
    return (
        attended.reshape(query_row.shape[0], -1).astype(jnp.bfloat16),
        (highest + jnp.log(totals))[..., 0],
    )


def attend_back(pieces):
    query_row, key_row, value_row, query_ids, key_ids, log_totals, grad_row = pieces
    query_heads = split_heads(query_row)
    key_heads = split_heads(key_row)
    value_heads = split_heads(value_row)
    grad_heads = split_heads(grad_row)
    logits = row_logits(query_heads, key_heads, query_ids, key_ids)
    probs = jnp.exp(logits - log_totals[..., None])
    probs_low = probs.astype(jnp.bfloat16)
    grad_probs = jnp.einsum(
        "qhd,khd->hqk", grad_heads, value_heads, preferred_element_type=jnp.float32
    )
    weighted = jnp.sum(probs * grad_probs, axis=-1, keepdims=True)
    grad_scores = (probs * (grad_probs - weighted)).astype(jnp.bfloat16)
    scale = HD ** (-0.5)
    grad_query = (
        jnp.einsum("hqk,khd->qhd", grad_scores, key_heads, preferred_element_type=jnp.float32)
        * scale
    )
    grad_key = (
        jnp.einsum("hqk,qhd->khd", grad_scores, query_heads, preferred_element_type=jnp.float32)
        * scale
    )
    grad_value = jnp.einsum(
        "hqk,qhd->khd", probs_low, grad_heads, preferred_element_type=jnp.float32
    )
    return (
        grad_query.reshape(query_row.shape[0], -1).astype(jnp.bfloat16),
        grad_key.reshape(key_row.shape[0], -1),
        grad_value.reshape(key_row.shape[0], -1),
    )


def local(
    grid,
    tokens,
    segment_ids,
    w_query,
    w_key,
    w_value,
    w_output,
    b_query,
    b_value,
    b_output,
    first_gain,
    first_shift,
    w_inner,
    b_inner,
    w_outer,
    b_outer,
    second_gain,
    second_shift,
    cotangent,
):
    rows_local, block_size, width = tokens.shape
    start = lax.axis_index("blk") * block_size
    query_ids = lax.dynamic_slice_in_dim(segment_ids, start, block_size, 1)
    valid = (query_ids > 0).astype(jnp.float32).reshape(-1, 1)
    flat = tokens.reshape(-1, width)
    small = (
        b_query, b_value, b_output, first_gain, first_shift, b_inner, b_outer, second_gain,
        second_shift,
    )
    sizes = [a.shape[0] for a in small]
    ends = [sum(sizes[: k + 1]) for k in range(len(sizes))]
    tile = -(-(ends[-1] + 3) // 1024) * 8
    packed = jnp.pad(jnp.concatenate(small), (0, tile * 128 - ends[-1])).reshape(tile, 128)
    shards = lax.axis_size("rows") * lax.axis_size("blk")
    hidden = w_inner.shape[1]
    inner_halves, outer_halves = halves(*w_inner.shape), halves(*w_outer.shape)
    one, two = ("z", "x", "y"), ("z", "y", "x")
    full, within = grid.order, grid.in_blk
    near = tuple(a for a in within if a != "c")
    got = gather(
        grid,
        (flat, packed, w_query, w_key, w_value, w_output, w_inner, w_outer),
        (within,) + (full,) * 7,
        (
            (1, None, one),
            (3, None, two),
            (4, None, one),
            (0, None, near),
            (2, None, two),
            (5, None, one),
            (6, inner_halves[0], two),
            (6, inner_halves[1], one),
            (7, outer_halves[0], two),
            (7, outer_halves[1], one),
        ),
        1,
    )
    tokens_all = got[0].reshape(-1, block_size, width)
    vectors = got[1].reshape(shards, -1)
    (
        bias_query, bias_value, bias_output, gain_one, shift_one, bias_inner, bias_outer, gain_two,
        shift_two,
    ) = (vectors[:, e - n : e].reshape(-1) for e, n in zip(ends, sizes))
    full_query, full_key, full_value, full_output = (
        g.reshape(-1, width) for g in got[2:6]
    )
    full_inner = got[6].reshape(-1, hidden)
    full_outer = got[7].reshape(-1, width)
    blocks = lax.axis_size("blk")

    def by_row(blocks_in):
        blocks_in = blocks_in.reshape(blocks, rows_local, block_size, width)
        return blocks_in.transpose(1, 0, 2, 3).reshape(rows_local, blocks * block_size, width)

    tokens_all = tokens_all.reshape(-1, width)
    keys_whole = by_row(plain_product(tokens_all, full_key).astype(jnp.bfloat16))
    values_whole = by_row(
        (plain_product(tokens_all, full_value) + bias_value).astype(jnp.bfloat16)
    )
    queries = (plain_product(flat, full_query) + bias_query).astype(jnp.bfloat16)
    queries = queries.reshape(rows_local, block_size, width)
    attended, log_totals = lax.map(
        attend_row, (queries, keys_whole, values_whole, query_ids, segment_ids)
    )
    attended_flat = attended.reshape(-1, width)
    branch = plain_product(attended_flat, full_output) + bias_output
    flat_wide = flat.astype(jnp.float32)
    stat_sums = (
        jnp.sum(valid * flat_wide * flat_wide),
        jnp.sum(valid * branch * branch),
        jnp.sum(valid),
    )
    first, first_back = jax.vjp(
        layer_norm, flat_wide + branch, gain_one.astype(jnp.float32), shift_one.astype(jnp.float32)
    )
    first_low = first.astype(jnp.bfloat16)
    inner = plain_product(first_low, full_inner) + bias_inner
    active_wide, gelu_back = jax.vjp(gelu_exact, inner)
    active = active_wide.astype(jnp.bfloat16)
    outer = plain_product(active, full_outer) + bias_outer
    result, second_back = jax.vjp(
        layer_norm, first + outer, gain_two.astype(jnp.float32), shift_two.astype(jnp.float32)
    )
    block_out = result.astype(jnp.bfloat16).reshape(tokens.shape)
    upstream = cotangent.reshape(-1, width).astype(jnp.float32) * valid
    grad_second, grad_gain_two, grad_shift_two = second_back(upstream)
    grad_outer = grad_second.astype(jnp.bfloat16)
    grad_bias_outer = jnp.sum(grad_outer.astype(jnp.float32), axis=0)
    grad_weight_outer = left_transpose(active, grad_outer)
    grad_active = right_transpose(grad_outer, full_outer)
    grad_inner = gelu_back(grad_active)[0].astype(jnp.bfloat16)
    grad_bias_inner = jnp.sum(grad_inner.astype(jnp.float32), axis=0)
    grad_weight_inner = left_transpose(first_low, grad_inner)
    grad_first = grad_second + right_transpose(grad_inner, full_inner)
    grad_resid, grad_gain_one, grad_shift_one = first_back(grad_first)
    grad_branch = grad_resid.astype(jnp.bfloat16)
    grad_bias_output = jnp.sum(grad_branch.astype(jnp.float32), axis=0)
    grad_weight_output = left_transpose(attended_flat, grad_branch)
    grad_attended = right_transpose(grad_branch, full_output).astype(jnp.bfloat16)
    grad_attended = grad_attended.reshape(rows_local, block_size, width)
    grad_queries, key_terms, value_terms = lax.map(
        attend_back,
        (queries, keys_whole, values_whole, query_ids, segment_ids, log_totals, grad_attended),
    )

    def by_block(terms):
        terms = terms.astype(jnp.bfloat16).reshape(rows_local, blocks, block_size, width)
        return terms.transpose(1, 0, 2, 3).reshape(
            *grid.dims(within), rows_local * block_size, width
        )

    backwards = ("c",) * ("c" in within) + near
    grad_key_flat, grad_value_flat = scatter(
        grid,
        (by_block(key_terms), by_block(value_terms)),
        (within, within),
        ((0, None, backwards), (1, None, backwards)),
        (jnp.bfloat16, jnp.bfloat16),
        2,
    )
    grad_query_flat = grad_queries.reshape(-1, width)
    grad_tokens = (
        grad_resid
        + right_transpose(grad_query_flat, full_query)
        + right_transpose(grad_key_flat, full_key)
        + right_transpose(grad_value_flat, full_value)
    )
    grad_weight_query = left_transpose(flat, grad_query_flat)
    grad_weight_key = left_transpose(flat, grad_key_flat)
    grad_weight_value = left_transpose(flat, grad_value_flat)
    grad_bias_query = jnp.sum(grad_query_flat.astype(jnp.float32), axis=0)
    grad_bias_value = jnp.sum(grad_value_flat.astype(jnp.float32), axis=0)
    sums = (
        grad_bias_query, grad_bias_value, grad_bias_output, grad_gain_one, grad_shift_one,
        grad_bias_inner, grad_bias_outer, grad_gain_two, grad_shift_two,
    )
    terms = jnp.concatenate(
        [g.reshape(shards, -1) for g in sums]
        + [jnp.broadcast_to(jnp.stack(stat_sums), (shards, 3))],
        axis=1,
    )
    terms = jnp.pad(terms, ((0, 0), (0, tile * 128 - ends[-1] - 3)))

    def parted(grad):
        return grad.astype(jnp.bfloat16).reshape(
            *grid.dims(full), grad.shape[0] // shards, grad.shape[1]
        )

    one, two = ("c", "x", "y", "z"), ("c", "y", "x", "z")
    shares = scatter(
        grid,
        (
            terms.reshape(*grid.dims(full), tile, 128),
            *(
                parted(g)
                for g in (
                    grad_weight_query, grad_weight_key, grad_weight_value, grad_weight_output,
                    grad_weight_inner, grad_weight_outer,
                )
            ),
        ),
        (full,) * 7,
        (
            (5, inner_halves[0], one),
            (5, inner_halves[1], two),
            (6, outer_halves[0], one),
            (6, outer_halves[1], two),
            (4, None, one),
            (1, None, two),
            (2, None, one),
            (3, None, two),
            (0, None, one),
        ),
        (jnp.float32,) * 7,
        3,
    )
    totals = shares[0].reshape(-1)
    small_shares = [totals[e - n : e] for e, n in zip(ends, sizes)]
    stat_totals = totals[ends[-1] : ends[-1] + 3]
    rms_tokens = jnp.sqrt(stat_totals[0] / (stat_totals[2] * width))
    rms_attention = jnp.sqrt(stat_totals[1] / (stat_totals[2] * width))
    return (
        block_out,
        grad_tokens.reshape(tokens.shape),
        *shares[1:5],
        *small_shares[:5],
        shares[5],
        small_shares[5],
        shares[6],
        *small_shares[6:],
        rms_tokens,
        rms_attention,
    )


def solution(mesh):
    placed = (
        P("rows", "blk", None),
        P("rows", None),
        P(("rows", "blk"), None),
        P(("rows", "blk"), None),
        P(("rows", "blk"), None),
        P(("rows", "blk"), None),
        P(("rows", "blk")),
        P(("rows", "blk")),
        P(("rows", "blk")),
        P(("rows", "blk")),
        P(("rows", "blk")),
        P(("rows", "blk"), None),
        P(("rows", "blk")),
        P(("rows", "blk"), None),
        P(("rows", "blk")),
        P(("rows", "blk")),
        P(("rows", "blk")),
        P("rows", "blk", None),
    )
    grid = Grid(mesh.shape["rows"], mesh.shape["blk"])
    return jax.shard_map(
        functools.partial(local, grid),
        mesh=mesh,
        in_specs=placed,
        out_specs=(
            P("rows", "blk", None),
            P("rows", "blk", None),
            P(("rows", "blk"), None),
            P(("rows", "blk"), None),
            P(("rows", "blk"), None),
            P(("rows", "blk"), None),
            P(("rows", "blk")),
            P(("rows", "blk")),
            P(("rows", "blk")),
            P(("rows", "blk")),
            P(("rows", "blk")),
            P(("rows", "blk"), None),
            P(("rows", "blk")),
            P(("rows", "blk"), None),
            P(("rows", "blk")),
            P(("rows", "blk")),
            P(("rows", "blk")),
            P(),
            P(),
        ),
        check_vma=False,
    )
```

time: 1230 us -> 342 us (0.28)
  waiting for transfers between devices: 987 us -> 0 us
  Pallas kernels: 0 us -> 188 us
  blocking collectives: 83.9 us -> 0 us
  between operations: 18.9 us -> 5.67 us
    reduce_scatter x5 -> x0, waiting for transfers between devices: 435 us -> none  [the longest x1 142 us: local(): lax.psum_scatter(grad_weight_inner, ('rows', 'blk'), scatter_dimension=0,...]
    all_gather x8 -> x0, waiting for transfers between devices: 307 us -> none  [the longest x1 63.3 us: local(): lax.all_gather(w_inner, ('rows', 'blk'), axis=0, tiled=True)]
    unnamed x19 -> x0, waiting for transfers between devices: 245 us -> none
    pallas_call x0 -> x3, Pallas kernels: none -> 188 us  [the longest x2 103 us: scatter(): pl.pallas_call(functools.partial(scatter_body, grid, axes_of, chunks, lag...]
    unnamed x2 -> x0, blocking collectives: 83.9 us -> none
    unnamed x112 -> x107, local copies, waits for them, and re-layouts: 24.1 us -> 9.41 us
    reshape x2 -> x16, local copies, waits for them, and re-layouts: 1.84 us -> 15.7 us  [the longest x4 9.43 us: by_block(): terms.astype(jnp.bfloat16).reshape(rows_local, blocks, block_size, width)]
    dynamic_update_slice x6 -> x2, local copies, waits for them, and re-layouts: 12.6 us -> 0.32 us  [local(): lax.map(attend_back, (queries, keys_whole, values_whole, query_ids, segme...]
  transfers between devices with their start and end apart: 16 -> 0, of which waited for: 16 -> 0; matrix products, arithmetic and copies ran while one was open for 7% -> 0% of each run, Pallas kernels for 0% -> 0%
where the time goes in v1:
time: 342 us; the launch traced here: 341 us
  Pallas kernels  188 us (55%)
  matrix products  66.3 us (19%)
  local copies, waits for them, and re-layouts  61 us (18%)
  other arithmetic  19.6 us (6%)
  between operations  5.67 us (2%)
    pallas_call x2, Pallas kernels, scatter(): pl.pallas_call(functools.partial(scatter_body, grid, axes_of, chunks, lag...  103 us
    pallas_call x1, Pallas kernels, gather(): pl.pallas_call(functools.partial(gather_body, grid, axes_of, chunks, ahea...  84.8 us
    dot_general x6, matrix products, plain_product(): return jnp.dot(left, right, preferred_element_type=jnp.float32)  25.9 us
    dot_general x6, matrix products, left_transpose(): lax.dot_general(left, right, (((0,), (0,)), ((), ())), preferred_element_...  14.8 us
    dot_general x6, matrix products, right_transpose(): lax.dot_general(left, right, (((1,), (1,)), ((), ())), preferred_element_...  14.6 us
    reshape x4, local copies, waits for them, and re-layouts, by_block(): terms.astype(jnp.bfloat16).reshape(rows_local, blocks, block_size, width)  9.43 us
    unnamed x107, local copies, waits for them, and re-layouts  9.41 us

profile of v1, /device:TPU:0, one launch (start us, length us, event | category | flops | bytes accessed | tf_op | source)
XLA Modules:
  0.0 340.9 jit_solution(653010603791830166)
XLA Ops:
  0.7 6.1 %concatenate.6 = bf16[288]{0:T(512)(128)(2,1)S(1)} concatenate(bf16[24]{0:T(256)(128)(2,1)} %param.28, bf16[24]{0:T(256)(128)(2,1)} %param.29, bf16[24]{0:T(256)(128)(2,1)} %param.30, bf16[24]{0:T(256)(128)(2,1)} %param.31, bf16[24]{0:T(256)(128)(2,1)} %param.32, bf16[96]{0:T(256)(128)(2,1)} %param.34, bf16[24]{0:T(256)(128)(2,1)} %param.36, bf16[24]{0:T(256)(128)(2,1)} %param.37, ...), dimensions={0} | concatenate | bytes 1152 | tf_op jit(solution)/shard_map/concatenate | solution.py:471
  7.3 84.8 %gather_1.1 = (bf16[2,2,256,768]{3,2,1,0:T(8,128)(2,1)}, bf16[4,2,2,2,8,128]{5,4,3,2,1,0:T(8,128)(2,1)}, bf16[4,2,2,2,24,768]{5,4,3,2,1,0:T(8,128)(2,1)}, bf16[4...) custom-call(bf16[256,768]{1,0:T(8,128)(2,1)} %bitcast.230, ...), custom_call_target="tpu_custom_call" | custom-call | tf_op jit(solution)/shard_map/gather_1/pallas_call | solution.py:187
  93.8 3.1 add_convert_fusion.1
  97.0 2.4 copy.46
  99.4 2.5 reshape.464
  103.4 3.1 convolution_convert_fusion.2
  106.5 2.2 copy.47
  108.8 2.5 reshape.469
  111.9 11.3 %while.26 = (s32[]{:T(128)}, bf16[2,128,768]{2,1,0:T(8,128)(2,1)}, f32[2,12,128]{2,1,0:T(8,128)}, bf16[2,512,768]{1,2,0:T(8,128)(2,1)S(1)}, s32[2,128]{1,0:T(2,1...) while((s32[]{:T(128)}, bf16[2,128,768]{2,1,0:T(8,128)(2,1)}, ...), condition=%wide.region_3.4_spmd, body=%wide.region_0.3_spmd.sunk | while | flops 210926080 | bytes 16050797 | solution.py:520
  112.1 0.9 constant_dynamic-slice_fusion.23
  115.3 1.3 fusion.110
  121.0 1.3 fusion.110
  124.0 2.8 fusion.32
  126.9 1.0 copy-done
  129.6 11.8 %multiply_convert_fusion.1 = (bf16[256,3072]{1,0:T(8,128)(2,1)}, f32[256,3072]{1,0:T(8,128)}, f32[256,3072]{1,0:T(8,128)}) fusion(f32[3072]{0:T(1024)S(1)} %reshape.504, bf16[768,3072]{1,0:T(8,128)(2,1)} %bitcast.267, f32[256,768]{1,0:T(8,128)} %copy-done, f32[768]{0:T(1024)S(1)} %reshape.503, f32[768]{0:T(1024)S(1)} %reshape.502, f32[256]{0:T(256)S(1)} %fusion.23, ...), kind=kOutput, calls=%fused_computation.45 | convolution fusion | flops 1260847104 | bytes 13389824 | tf_op jit(solution)/shard_map/dot_general | solution.py:363
  142.1 4.6 %fusion.35 = (f32[256]{0:T(256)S(1)}, f32[256,768]{1,0:T(8,128)S(1)}) fusion(f32[768]{0:T(1024)} %reshape.505, bf16[256,3072]{1,0:T(8,128)(2,1)} %get-tuple-element.256, bf16[3072,768]{1,0:T(8,128)(2,1)} %bitcast.271, f32[768]{0:T(1024)S(1)} %reshape.503, f32[768]{0:T(1024)S(1)} %reshape.502, f32[256]{0:T(256)} %copy-done.38, f32[256,768]{1,0:T(8,128)} %copy-done, ...), kind=kOutput, calls=%fused_computation.132 | convolution fusion | flops 1209335552 | bytes 7876608 | tf_op jit(solution)/shard_map/dot_general | solution.py:363
  149.2 1.2 compare_convert_fusion
  150.9 2.5 multiply_reduce_fusion.2
  153.4 1.3 multiply_multiply_fusion.8
  154.6 1.4 reshape.507
  156.0 2.4 fusion.30
  158.6 3.9 %convolution_convert_fusion = bf16[3072,768]{1,0:T(8,128)(2,1)} fusion(bf16[256,3072]{1,0:T(8,128)(2,1)S(1)} %copy-done.12, bf16[256,768]{1,0:T(8,128)(2,1)S(1)} %get-tuple-element.247), kind=kOutput, calls=%fused_computation.38 | convolution fusion | flops 1210318848 | bytes 6684672 | tf_op jit(solution)/shard_map/dot_general | solution.py:367
  162.5 6.0 %convert_reduce_fusion = (f32[3072]{0:T(1024)}, bf16[256,3072]{1,0:T(8,128)(2,1)S(1)}) fusion(f32[256,3072]{1,0:T(8,128)S(1)} %copy-done.52, f32[256,3072]{1,0:T(8,128)S(1)} %copy-done.53, bf16[256,768]{1,0:T(8,128)(2,1)S(1)} %get-tuple-element.247, bf16[3072,768]{1,0:T(8,128)(2,1)} %bitcast.272), kind=kOutput, calls=%fused_computation.43 | convolution fusion | flops 1220539392 | bytes 12988416 | tf_op jit(solution)/shard_map/dot_general | solution.py:373
  168.5 3.8 %convolution_convert_fusion.1 = bf16[768,3072]{1,0:T(8,128)(2,1)} fusion(bf16[256,3072]{1,0:T(8,128)(2,1)S(1)} %get-tuple-element.249, f32[256,768]{1,0:T(8,128)S(1)} %copy-done.1, f32[768]{0:T(1024)S(1)} %reshape.503, f32[768]{0:T(1024)S(1)} %reshape.502, f32[256]{0:T(256)S(1)} %copy-done.39, f32[256]{0:T(256)S(1)} %copy-done.35), kind=kOutput, calls=%fused_computation.39 | convolution fusion | flops 1211301888 | bytes 7086080 | tf_op jit(solution)/shard_map/dot_general | solution.py:367
  172.3 2.3 multiply_reduce_fusion.3
  176.0 1.6 convolution_convert_fusion.3
  177.6 1.3 convolution_convert_fusion.6
  178.9 19.7 %while.27 = (s32[]{:T(128)}, bf16[2,128,768]{1,2,0:T(8,128)(2,1)}, bf16[2,512,768]{1,2,0:T(8,128)(2,1)}, bf16[2,512,768]{1,2,0:T(8,128)(2,1)}, bf16[2,512,768]{1...) while((s32[]{:T(128)}, bf16[2,128,768]{1,2,0:T(8,128)(2,1)}, ...), condition=%wide.region_14.15_spmd, body=%wide.region_12.14_spmd.sunk | while | flops 511441408 | bytes 64857948 | solution.py:559
  182.5 1.3 multiply_reduce_fusion.9
  192.4 1.3 multiply_reduce_fusion.9
  198.6 2.4 reshape.477
  200.9 2.4 copy.53
  203.4 2.4 reshape.479
  205.8 2.3 copy.54
  208.1 23.5 %scatter_2.1 = (bf16[256,768]{1,0:T(8,128)(2,1)}, bf16[256,768]{1,0:T(8,128)(2,1)}) custom-call(bf16[2,2,256,768]{3,2,1,0:T(8,128)(2,1)} %bitcast.234, bf16[2,2,256,768]{3,2,1,0:T(8,128)(2,1)} %bitcast.235), custom_call_target="tpu_custom_call" | custom-call | tf_op jit(solution)/shard_map/scatter_2/pallas_call | solution.py:330
  231.6 1.1 convert_reduce_fusion.3
  233.6 1.0 fusion.19
  234.7 2.0 pad_maximum_fusion
  237.7 2.5 convolution_convert_fusion.5
  240.2 1.6 convolution_convert_fusion.4
  241.8 1.5 bitcast_convert_fusion
  243.3 79.7 %scatter_3.1 = (f32[8,128]{1,0:T(8,128)}, f32[24,768]{1,0:T(8,128)}, f32[24,768]{1,0:T(8,128)}, f32[24,768]{1,0:T(8,128)}, f32[24,768]{1,0:T(8,128)}, /*index=5*/f32[24,3072]{1,0:T(8,128)}, f32[96,768]{1,0:T(8,128)}) custom-call(f32[4,2,2,2,8,128]{5,4,3,2,1,0:T(8,128)} %bitcast.256, bf16[4,2,2,2,24,768]{5,4,3,2,1,0:T(8,128)(2,1)} %bitcast.241, ...), custom_call_target="tpu_custom_call" | custom-call | tf_op jit(solution)/shard_map/scatter_3/pallas_call | solution.py:330
  323.0 1.4 fusion.33
  326.4 1.6 fusion.34
  328.0 1.3 slice.82
  329.5 1.9 convolution_add_fusion.4
  331.4 1.9 convolution_add_fusion.3
  333.3 1.4 convolution_add_fusion.2
  (230 shorter events, 42.5 us)
Async XLA Ops:
  96.9 5.0 %copy-start.2 = (bf16[2,128,768]{2,1,0:T(8,128)(2,1)S(1)}, bf16[2,128,768]{2,1,0:T(8,128)(2,1)}, u32[]{:S(2)}) copy-start(bf16[2,128,768]{2,1,0:T(8,128)(2,1)} %param.22) | copy-start | bytes 1179652
  97.0 5.0 %copy-start.22 = (bf16[4,2,2,2,24,768]{5,4,3,2,1,0:T(8,128)(2,1)S(1)}, bf16[4,2,2,2,24,768]{5,4,3,2,1,0:T(8,128)(2,1)}, u32[]{:S(2)}) copy-start(bf16[4,2,2,2,24,768]{5,4,3,2,1,0:T(8,128)(2,1)} %get-tuple-element.141) | copy-start | bytes 3538948
  106.5 4.7 %copy-start.26 = (s32[2,512]{1,0:T(2,128)S(1)}, s32[2,512]{1,0:T(2,128)}, u32[]{:S(2)}) copy-start(s32[2,512]{1,0:T(2,128)} %param.23) | copy-start | bytes 12292
  123.2 4.9 %copy-start.50 = (s32[2,128]{1,0:T(2,128)}, s32[2,128]{1,0:T(2,128)S(1)}, u32[]{:S(2)}) copy-start(s32[2,128]{1,0:T(2,128)S(1)} %get-tuple-element.531) | copy-start | bytes 3076
  123.2 4.9 %copy-start.33 = (f32[32,24]{1,0:T(8,128)S(1)}, f32[32,24]{1,0:T(8,128)}, u32[]{:S(2)}) copy-start(f32[32,24]{1,0:T(8,128)} %get-tuple-element.273) | copy-start | bytes 9220
  123.2 5.4 %copy-start.32 = (f32[32,24]{1,0:T(8,128)S(1)}, f32[32,24]{1,0:T(8,128)}, u32[]{:S(2)}) copy-start(f32[32,24]{1,0:T(8,128)} %get-tuple-element.272) | copy-start | bytes 9220
  126.9 15.2 %copy-start.34 = (f32[256]{0:T(256)}, f32[256]{0:T(256)S(1)}, u32[]{:S(2)}) copy-start(f32[256]{0:T(256)S(1)} %broadcast_multiply_fusion.1) | copy-start | bytes 3076
  128.1 13.3 %copy-start.38 = (f32[256]{0:T(256)}, f32[256]{0:T(256)S(1)}, u32[]{:S(2)}) copy-start(f32[256]{0:T(256)S(1)} %fusion.23) | copy-start | bytes 3076
  129.6 11.8 %copy-start.31 = (f32[32,24]{1,0:T(8,128)S(1)}, f32[32,24]{1,0:T(8,128)}, u32[]{:S(2)}) copy-start(f32[32,24]{1,0:T(8,128)} %get-tuple-element.271) | copy-start | bytes 9220
  142.1 8.8 %copy-start.13 = (bf16[2,128,768]{2,1,0:T(8,128)(2,1)S(1)}, bf16[2,128,768]{2,1,0:T(8,128)(2,1)}, u32[]{:S(2)}) copy-start(bf16[2,128,768]{2,1,0:T(8,128)(2,1)} %param.39) | copy-start | bytes 1179652
  146.7 1.7 copy-start.36
  156.0 2.6 copy-start.12
  158.5 4.0 %copy-start.53 = (f32[256,3072]{1,0:T(8,128)S(1)}, f32[256,3072]{1,0:T(8,128)}, u32[]{:S(2)}) copy-start(f32[256,3072]{1,0:T(8,128)} %get-tuple-element.291) | copy-start | bytes 9437188
  158.6 3.9 %copy-start.52 = (f32[256,3072]{1,0:T(8,128)S(1)}, f32[256,3072]{1,0:T(8,128)}, u32[]{:S(2)}) copy-start(f32[256,3072]{1,0:T(8,128)} %get-tuple-element.257) | copy-start | bytes 9437188
  158.6 13.7 %slice-start = ((s8[4718592]{0:T(1024)(128)(4,1)}), s8[4194304]{0:T(1024)(128)(4,1)S(1)}, s32[]{:S(2)}) async-start(s8[4718592]{0:T(1024)(128)(4,1)} %bitcast.268), calls=%async_computation | async-start | bytes 8388608
  162.5 6.0 %copy-start.1 = (f32[256,768]{1,0:T(8,128)S(1)}, f32[256,768]{1,0:T(8,128)}, u32[]{:S(2)}) copy-start(f32[256,768]{1,0:T(8,128)} %copy-done) | copy-start | bytes 2359300
  162.5 6.0 %copy-start.35 = (f32[256]{0:T(256)S(1)}, f32[256]{0:T(256)}, u32[]{:S(2)}) copy-start(f32[256]{0:T(256)} %copy-done.34) | copy-start | bytes 3076
  162.5 6.0 %copy-start.39 = (f32[256]{0:T(256)S(1)}, f32[256]{0:T(256)}, u32[]{:S(2)}) copy-start(f32[256]{0:T(256)} %copy-done.38) | copy-start | bytes 3076
  162.5 9.8 %slice-start.1 = ((s8[4718592]{0:T(1024)(128)(4,1)}), s8[524288]{0:T(1024)(128)(4,1)S(1)}, s32[]{:S(2)}) async-start(s8[4718592]{0:T(1024)(128)(4,1)} %bitcast.268), calls=%async_computation.1 | async-start | bytes 1048576
  172.3 2.3 copy-start.43
  174.6 3.0 copy-start.7
  175.0 3.9 %copy-start.45 = (f32[256]{0:T(256)}, f32[256]{0:T(256)S(1)}, u32[]{:S(2)}) copy-start(f32[256]{0:T(256)S(1)} %negate_multiply_fusion.1) | copy-start | bytes 3076
  184.2 1.4 copy-start.15
  184.2 1.9 copy-start.17
  185.0 2.9 copy-start.9
  186.3 1.6 copy-start.18
  194.1 1.9 copy-start.17
  194.9 2.9 copy-start.9
  196.1 1.6 copy-start.18
  205.7 27.1 %copy-start.11 = (bf16[2,128,768]{1,2,0:T(8,128)(2,1)S(1)}, bf16[2,128,768]{1,2,0:T(8,128)(2,1)}, u32[]{:S(2)}) copy-start(bf16[2,128,768]{1,2,0:T(8,128)(2,1)} %get-tuple-element.148) | copy-start | bytes 1179652
  205.8 27.5 %copy-start.49 = (f32[768]{0:T(1024)S(1)}, f32[768]{0:T(1024)}, u32[]{:S(2)}) copy-start(f32[768]{0:T(1024)} %get-tuple-element.198) | copy-start | bytes 9220
  205.8 27.6 %copy-start.48 = (f32[768]{0:T(1024)S(1)}, f32[768]{0:T(1024)}, u32[]{:S(2)}) copy-start(f32[768]{0:T(1024)} %get-tuple-element.202) | copy-start | bytes 9220
  205.8 27.6 %copy-start.40 = (f32[3072]{0:T(1024)S(1)}, f32[3072]{0:T(1024)}, u32[]{:S(2)}) copy-start(f32[3072]{0:T(1024)} %get-tuple-element.248) | copy-start | bytes 36868
  205.8 27.8 %copy-start.3 = (bf16[2,128,768]{2,1,0:T(8,128)(2,1)S(1)}, bf16[2,128,768]{2,1,0:T(8,128)(2,1)}, u32[]{:S(2)}) copy-start(bf16[2,128,768]{2,1,0:T(8,128)(2,1)} %param.22) | copy-start | bytes 1179652
  205.8 27.8 %copy-start.14 = (bf16[2,128,768]{2,1,0:T(8,128)(2,1)S(1)}, bf16[2,128,768]{2,1,0:T(8,128)(2,1)}, u32[]{:S(2)}) copy-start(bf16[2,128,768]{2,1,0:T(8,128)(2,1)} %param.39) | copy-start | bytes 1179652
  205.8 27.8 %copy-start.47 = (f32[2,128]{1,0:T(2,128)S(1)}, f32[2,128]{1,0:T(2,128)}, u32[]{:S(2)}) copy-start(f32[2,128]{1,0:T(2,128)} %get-tuple-element.288) | copy-start | bytes 3076
  208.1 28.6 %copy-start.37 = (f32[768]{0:T(1024)S(1)}, f32[768]{0:T(1024)}, u32[]{:S(2)}) copy-start(f32[768]{0:T(1024)} %get-tuple-element.200) | copy-start | bytes 9220
  231.6 8.6 %copy-start.8 = (bf16[256,768]{1,0:T(8,128)(2,1)S(1)}, bf16[256,768]{1,0:T(8,128)(2,1)}, u32[]{:S(2)}) copy-start(bf16[256,768]{1,0:T(8,128)(2,1)} %get-tuple-element.152) | copy-start | bytes 1179652
  243.3 86.1 %copy-start.6 = (f32[256,768]{1,0:T(8,128)S(1)}, f32[256,768]{1,0:T(8,128)}, u32[]{:S(2)}) copy-start(f32[256,768]{1,0:T(8,128)} %copy-done.5) | copy-start | bytes 2359300
  243.3 86.2 %copy-start.46 = (f32[256]{0:T(256)S(1)}, f32[256]{0:T(256)}, u32[]{:S(2)}) copy-start(f32[256]{0:T(256)} %copy-done.45) | copy-start | bytes 3076
  323.0 8.4 %copy-start.19 = (bf16[256,768]{1,0:T(8,128)(2,1)S(1)}, bf16[256,768]{1,0:T(8,128)(2,1)}, u32[]{:S(2)}) copy-start(bf16[256,768]{1,0:T(8,128)(2,1)} %get-tuple-element.151) | copy-start | bytes 1179652
  329.5 3.8 %copy-start.21 = (bf16[4,2,2,2,24,768]{5,4,3,2,1,0:T(8,128)(2,1)S(1)}, bf16[4,2,2,2,24,768]{5,4,3,2,1,0:T(8,128)(2,1)}, u32[]{:S(2)}) copy-start(bf16[4,2,2,2,24,768]{5,4,3,2,1,0:T(8,128)(2,1)} %get-tuple-element.139) | copy-start | bytes 3538948
  331.4 3.3 copy-start.30
  331.4 4.0 %copy-start.29 = (f32[24,768]{1,0:T(8,128)S(1)}, f32[24,768]{1,0:T(8,128)}, u32[]{:S(2)}) copy-start(f32[24,768]{1,0:T(8,128)} %get-tuple-element.512) | copy-start | bytes 221188
  331.4 4.6 %copy-start.28 = (f32[24,768]{1,0:T(8,128)S(1)}, f32[24,768]{1,0:T(8,128)}, u32[]{:S(2)}) copy-start(f32[24,768]{1,0:T(8,128)} %get-tuple-element.513) | copy-start | bytes 221188
  331.4 5.2 %copy-start.27 = (f32[24,768]{1,0:T(8,128)S(1)}, f32[24,768]{1,0:T(8,128)}, u32[]{:S(2)}) copy-start(f32[24,768]{1,0:T(8,128)} %get-tuple-element.514) | copy-start | bytes 221188
  331.4 5.8 %copy-start.25 = (f32[24,3072]{1,0:T(8,128)S(1)}, f32[24,3072]{1,0:T(8,128)}, u32[]{:S(2)}) copy-start(f32[24,3072]{1,0:T(8,128)} %get-tuple-element.520) | copy-start | bytes 884740
  331.4 6.5 %copy-start.24 = (f32[96,768]{1,0:T(8,128)S(1)}, f32[96,768]{1,0:T(8,128)}, u32[]{:S(2)}) copy-start(f32[96,768]{1,0:T(8,128)} %get-tuple-element.522) | copy-start | bytes 884740
  (15 other events, 13.4 us)

commit v2 on v1

--- a/solution.py
+++ b/solution.py
@@ -10,6 +10,7 @@
 
 HEADS = 12
 HD = 64
+WIDTH = HEADS * HD
 EVERY = slice(None)
 MESH = pl.DeviceIdType.MESH
 
@@ -84,106 +85,135 @@
     return (1, 0, columns // 2), (1, columns // 2, columns // 2)
 
 
-def gather_body(grid, axes_of, chunks, ahead, lags, *refs):
-    n = len(axes_of)
-    ins, outs = refs[:n], refs[n : 2 * n]
-    send_sem, recv_sem, core_send, core_recv, keep_sem = refs[2 * n :]
-    me = grid.here()
-    grid.greet(me, grid.order)
-    sibling = grid.device(grid.toward(me, "c", 1))
-    other = grid.toward(me, "c", 1)["c"]
-    sent = []
-
-    def lead(i, **over):
-        return tuple(over.get(a, me[a]) for a in axes_of[i])
-
-    kept = []
-    for i in range(n):
-        copy = pltpu.make_async_copy(ins[i], outs[i].at[lead(i)], keep_sem.at[i])
-        copy.start()
-        kept.append(copy)
-
-    def ship(t, j, start):
-        i, cut, phases = chunks[t]
-        axis = phases[j]
+class Gather:
+    def __init__(self, grid, axes_of, chunks, ahead, lags, ins, outs, sems):
+        self.grid, self.axes_of, self.chunks, self.ahead = grid, axes_of, chunks, ahead
+        self.ins, self.outs = ins, outs
+        self.send_sem, self.recv_sem, self.core_send, self.core_recv, self.keep_sem = sems
+        self.me = grid.here()
+        grid.greet(self.me, grid.order)
+        across = grid.toward(self.me, "c", 1)
+        self.sibling, self.other = grid.device(across), across["c"]
+        self.sent, self.kept, self.step = [], [], 0
+        for i in range(len(axes_of)):
+            copy = pltpu.make_async_copy(ins[i], outs[i].at[self.lead(i)], self.keep_sem.at[i])
+            copy.start()
+            self.kept.append(copy)
+        for t in range(min(ahead, len(chunks))):
+            self.begin(t)
+        for copy in self.kept:
+            copy.wait()
+        self.stages = max(len(c[2]) for c in chunks)
+        self.starts = [sum(lags[:j]) for j in range(self.stages)]
+
+    def lead(self, i, **over):
+        return tuple(over.get(a, self.me[a]) for a in self.axes_of[i])
+
+    def begin(self, t):
+        self.ship(t, 0, True)
+        self.pass_on(t, 0, True)
+
+    def ship(self, t, j, start):
+        i, cut, phases = self.chunks[t]
+        grid, me, axis = self.grid, self.me, phases[j]
         got = {a: EVERY for a in phases[:j]}
-        mine = piece(outs[i], lead(i, **got), cut)
-        source = piece(ins[i], (), cut) if j == 0 else mine
+        mine = piece(self.outs[i], self.lead(i, **got), cut)
+        source = piece(self.ins[i], (), cut) if j == 0 else mine
         for k in range(1, grid.size[axis]):
-            sems = send_sem.at[t, j, k - 1], recv_sem.at[t, j, k - 1]
+            sems = self.send_sem.at[t, j, k - 1], self.recv_sem.at[t, j, k - 1]
             if start:
                 copy = pltpu.make_async_remote_copy(
                     source, mine, *sems,
                     device_id=grid.device(grid.toward(me, axis, k)), device_id_type=MESH,
                 )
                 copy.start()
-                sent.append(copy)
+                self.sent.append(copy)
             else:
-                theirs = piece(outs[i], lead(i, **got, **{axis: grid.away(me, axis, k)}), cut)
+                place = {**got, axis: grid.away(me, axis, k)}
+                theirs = piece(self.outs[i], self.lead(i, **place), cut)
                 pltpu.make_async_remote_copy(
-                    source, theirs, *sems, device_id=sibling, device_id_type=MESH
+                    source, theirs, *sems, device_id=self.sibling, device_id_type=MESH
                 ).wait_recv()
 
-    def pass_on(t, j, start):
-        i, cut, phases = chunks[t]
-        if "c" not in axes_of[i]:
+    def pass_on(self, t, j, start):
+        i, cut, phases = self.chunks[t]
+        if "c" not in self.axes_of[i]:
             return
-        if j == 0:
-            places = [{}]
-        else:
+        places = [{}]
+        if j > 0:
             axis = phases[j - 1]
             got = {a: EVERY for a in phases[: j - 1]}
-            places = [{**got, axis: grid.away(me, axis, k)} for k in range(1, grid.size[axis])]
+            places = [
+                {**got, axis: self.grid.away(self.me, axis, k)}
+                for k in range(1, self.grid.size[axis])
+            ]
         for p, place in enumerate(places):
-            mine = piece(outs[i], lead(i, **place), cut)
-            sems = core_send.at[t, j, p], core_recv.at[t, j, p]
+            mine = piece(self.outs[i], self.lead(i, **place), cut)
+            sems = self.core_send.at[t, j, p], self.core_recv.at[t, j, p]
             if start:
-                source = piece(ins[i], (), cut) if j == 0 else mine
+                source = piece(self.ins[i], (), cut) if j == 0 else mine
                 copy = pltpu.make_async_remote_copy(
-                    source, mine, *sems, device_id=sibling, device_id_type=MESH
+                    source, mine, *sems, device_id=self.sibling, device_id_type=MESH
                 )
                 copy.start()
-                sent.append(copy)
+                self.sent.append(copy)
             else:
-                theirs = piece(outs[i], lead(i, **place, c=other), cut)
+                theirs = piece(self.outs[i], self.lead(i, **place, c=self.other), cut)
                 pltpu.make_async_remote_copy(
-                    mine, theirs, *sems, device_id=sibling, device_id_type=MESH
+                    mine, theirs, *sems, device_id=self.sibling, device_id_type=MESH
                 ).wait_recv()
 
-    count = len(chunks)
-
-    def begin(t):
-        ship(t, 0, True)
-        pass_on(t, 0, True)
-
-    for t in range(min(ahead, count)):
-        begin(t)
-    for copy in kept:
-        copy.wait()
-    stages = max(len(c[2]) for c in chunks)
-    starts = [sum(lags[:j]) for j in range(stages)]
-    for s in range(count + starts[-1]):
-        if s + ahead < count:
-            begin(s + ahead)
-        for j in range(stages):
-            t = s - starts[j]
-            if 0 <= t < count and j < len(chunks[t][2]):
-                ship(t, j, False)
-                if j + 1 < len(chunks[t][2]):
-                    ship(t, j + 1, True)
-                pass_on(t, j + 1, True)
-    for t in range(count):
-        for j in range(len(chunks[t][2]) + 1):
-            pass_on(t, j, False)
-    for copy in sent:
-        copy.wait_send()
-
-
-def gather(grid, arrays, axes_of, chunks, ident, ahead=4, lags=(1, 3, 3)):
-    count = len(chunks)
-    widest = max(grid.size.values())
+    def advance(self, until):
+        count = len(self.chunks)
+        last = count + self.starts[-1]
+        while self.step < (last if until is None else min(until, last)):
+            s = self.step
+            if s + self.ahead < count:
+                self.begin(s + self.ahead)
+            for j in range(self.stages):
+                t = s - self.starts[j]
+                if 0 <= t < count and j < len(self.chunks[t][2]):
+                    self.ship(t, j, False)
+                    if j + 1 < len(self.chunks[t][2]):
+                        self.ship(t, j + 1, True)
+                    self.pass_on(t, j + 1, True)
+            self.step += 1
+
+    def arrived(self, t):
+        self.advance(t + self.starts[len(self.chunks[t][2]) - 1] + 1)
+        for j in range(len(self.chunks[t][2]) + 1):
+            self.pass_on(t, j, False)
+
+    def finish(self):
+        for copy in self.sent:
+            copy.wait_send()
+
+
+def gather_sems(grid, arrays, chunks):
+    count, widest = len(chunks), max(grid.size.values())
     stages = max(len(c[2]) for c in chunks)
     dma = pltpu.SemaphoreType.DMA
+    return [
+        dma((count, stages, widest - 1)),
+        dma((count, stages, widest - 1)),
+        dma((count, stages + 1, widest - 1)),
+        dma((count, stages + 1, widest - 1)),
+        dma((arrays,)),
+    ]
+
+
+def gather_body(grid, axes_of, chunks, ahead, lags, *refs):
+    n = len(axes_of)
+    run = Gather(
+        grid, axes_of, chunks, ahead, lags, refs[:n], refs[n : 2 * n], refs[2 * n :]
+    )
+    run.advance(None)
+    for t in range(len(chunks)):
+        run.arrived(t)
+    run.finish()
+
+
+def gather(grid, arrays, axes_of, chunks, ident, ahead=4, lags=(1, 3, 3)):
     return pl.pallas_call(
         functools.partial(gather_body, grid, axes_of, chunks, ahead, lags),
         out_shape=[
@@ -192,13 +222,7 @@
         ],
         in_specs=[pl.BlockSpec(memory_space=pltpu.VMEM)] * len(arrays),
         out_specs=[pl.BlockSpec(memory_space=pl.ANY)] * len(arrays),
-        scratch_shapes=[
-            dma((count, stages, widest - 1)),
-            dma((count, stages, widest - 1)),
-            dma((count, stages + 1, widest - 1)),
-            dma((count, stages + 1, widest - 1)),
-            dma((len(arrays),)),
-        ],
+        scratch_shapes=gather_sems(grid, len(arrays), chunks),
         compiler_params=pltpu.CompilerParams(collective_id=ident, has_side_effects=True),
         name="gather_" + str(ident),
     )(*arrays)
@@ -435,6 +459,135 @@
     )
 
 
+def halves_apart(pair):
+    low = lax.broadcasted_iota(jnp.int32, pair.shape, 1) < HD
+    none = jnp.zeros_like(pair)
+    return jnp.concatenate([jnp.where(low, pair, none), jnp.where(low, none, pair)], axis=0)
+
+
+def halves_joined(both):
+    n = both.shape[0] // 2
+    low = lax.broadcasted_iota(jnp.int32, (n, both.shape[1]), 1) < HD
+    return jnp.where(low, both[:n], both[n:])
+
+
+def masked_pair(query_pair, key_pair, same):
+    scores = right_transpose(query_pair, key_pair) * HD ** (-0.5)
+    n = same.shape[0]
+    return jnp.where(same[None], scores.reshape(2, n, -1), MASKED).reshape(2 * n, -1)
+
+
+def forward_body(grid, axes_of, chunks, ahead, lags, *refs):
+    n = len(axes_of)
+    ins = refs[:n]
+    column_ids, row_ids = refs[n : n + 2]
+    outs = refs[n + 2 : 2 * n + 1]
+    vectors, bias_inner, queries, keys, values, attended, log_totals, branch = refs[
+        2 * n + 1 : 2 * n + 9
+    ]
+    tokens_all = refs[2 * n + 9]
+    run = Gather(
+        grid, axes_of, chunks, ahead, lags, ins, (tokens_all, *outs), refs[2 * n + 10 :]
+    )
+    packed, w_query, w_key, w_value, w_output = outs[:5]
+    width = queries.shape[1]
+    blocks, block_rows = keys.shape[0], keys.shape[1]
+    rows_local = row_ids.shape[0]
+    block = block_rows // rows_local
+
+    run.arrived(0)
+    run.arrived(1)
+    run.arrived(2)
+    run.arrived(3)
+    shards = math.prod(grid.dims(grid.order))
+    flat_packed = packed.reshape(shards, *packed.shape[-2:])
+    part, part_inner = width // shards, bias_inner.shape[1] // shards
+    for s in range(shards):
+        vectors[:, part * s : part * (s + 1)] = flat_packed[s][:, 0:part]
+        bias_inner[:, part_inner * s : part_inner * (s + 1)] = flat_packed[s][5:6, 0:part_inner]
+    flat_tokens = tokens_all.reshape(blocks, block_rows, width)
+
+    def project(b, carry):
+        block_in = flat_tokens[b]
+        keys[b] = plain_product(block_in, w_key[...].reshape(width, width)).astype(keys.dtype)
+        made = plain_product(block_in, w_value[...].reshape(width, width)) + vectors[1:2, :]
+        values[b] = made.astype(values.dtype)
+        return carry
+
+    lax.fori_loop(0, blocks, project, 0)
+    run.arrived(4)
+    made = plain_product(ins[0][...], w_query[...].reshape(width, width)) + vectors[0:1, :]
+    queries[...] = made.astype(queries.dtype)
+
+    def attend(r):
+        mine = slice(r * block, (r + 1) * block)
+        same = column_ids[mine, :] == row_ids[r]
+        lane = lax.broadcasted_iota(jnp.int32, (block, 128), 1)
+
+        def pair(p, totals_so_far):
+            lanes = pl.ds(pl.multiple_of(p * 128, 128), 128)
+            logits = masked_pair(
+                halves_apart(queries[mine, lanes]),
+                keys[:, mine, lanes].reshape(blocks * block, 128),
+                same,
+            )
+            highest = jnp.max(logits, axis=-1, keepdims=True)
+            raised = jnp.exp(logits - highest)
+            totals = jnp.sum(raised, axis=-1, keepdims=True)
+            probs_low = (raised * (1.0 / totals)).astype(jnp.bfloat16)
+            both = plain_product(probs_low, values[:, mine, lanes].reshape(blocks * block, 128))
+            attended[mine, lanes] = halves_joined(both).astype(attended.dtype)
+            found = highest + jnp.log(totals)
+            totals_so_far = jnp.where(lane == 2 * p, found[:block], totals_so_far)
+            return jnp.where(lane == 2 * p + 1, found[block:], totals_so_far)
+
+        log_totals[mine, :] = lax.fori_loop(
+            0, HEADS // 2, pair, jnp.zeros((block, 128), jnp.float32)
+        )
+
+    for r in range(rows_local):
+        run.advance(run.step + 1)
+        attend(r)
+    run.arrived(5)
+    branch[...] = plain_product(attended[...], w_output[...].reshape(width, width)) + vectors[2:3, :]
+    run.advance(None)
+    for t in range(6, len(chunks)):
+        run.arrived(t)
+    run.finish()
+
+
+def forward(grid, arrays, axes_of, chunks, column_ids, row_ids, hidden, ident, ahead=4, lags=(1, 3, 3)):
+    block_rows, width = arrays[0].shape
+    blocks = math.prod(grid.dims(grid.in_blk))
+    low, wide = jnp.bfloat16, jnp.float32
+    shape = jax.ShapeDtypeStruct
+    found = [shape((*grid.dims(x), *a.shape), a.dtype) for a, x in zip(arrays, axes_of)]
+    vmem, anywhere = pl.BlockSpec(memory_space=pltpu.VMEM), pl.BlockSpec(memory_space=pl.ANY)
+    return pl.pallas_call(
+        functools.partial(forward_body, grid, axes_of, chunks, ahead, lags),
+        out_shape=[
+            *found[1:],
+            shape((arrays[1].shape[0], width), wide),
+            shape((1, hidden), wide),
+            shape((block_rows, width), low),
+            shape((blocks, block_rows, width), low),
+            shape((blocks, block_rows, width), low),
+            shape((block_rows, width), low),
+            shape((block_rows, 128), wide),
+            shape((block_rows, width), wide),
+        ],
+        in_specs=[vmem] * (len(arrays) + 2),
+        out_specs=[vmem] * 5 + [anywhere] * 2 + [vmem] * 8,
+        scratch_shapes=[
+            pltpu.VMEM(found[0].shape, low), *gather_sems(grid, len(arrays), chunks)
+        ],
+        compiler_params=pltpu.CompilerParams(
+            collective_id=ident, has_side_effects=True, vmem_limit_bytes=60 * 2**20
+        ),
+        name="forward",
+    )(*arrays, column_ids, row_ids)
+
+
 def local(
     grid,
     tokens,
@@ -651,6 +804,216 @@
     )
 
 
+def local_fused(
+    grid,
+    tokens,
+    segment_ids,
+    w_query,
+    w_key,
+    w_value,
+    w_output,
+    b_query,
+    b_value,
+    b_output,
+    first_gain,
+    first_shift,
+    w_inner,
+    b_inner,
+    w_outer,
+    b_outer,
+    second_gain,
+    second_shift,
+    cotangent,
+):
+    rows_local, block_size, width = tokens.shape
+    start = lax.axis_index("blk") * block_size
+    query_ids = lax.dynamic_slice_in_dim(segment_ids, start, block_size, 1)
+    valid = (query_ids > 0).astype(jnp.float32).reshape(-1, 1)
+    flat = tokens.reshape(-1, width)
+    small = (
+        b_query, b_value, b_output, first_gain, first_shift, b_inner, b_outer, second_gain,
+        second_shift,
+    )
+    sizes = [a.shape[0] for a in small]
+    ends = [sum(sizes[: k + 1]) for k in range(len(sizes))]
+    tile = -(-(ends[-1] + 3) // 1024) * 8
+    packed = jnp.stack(
+        [jnp.pad(a.astype(jnp.float32), (0, 128 - a.shape[0])) for a in small]
+    )
+    packed = jnp.pad(packed, ((0, 16 - len(small)), (0, 0)))
+    shards = lax.axis_size("rows") * lax.axis_size("blk")
+    blocks = lax.axis_size("blk")
+    hidden = w_inner.shape[1]
+    inner_halves, outer_halves = halves(*w_inner.shape), halves(*w_outer.shape)
+    one, two = ("z", "x", "y"), ("z", "y", "x")
+    full, within = grid.order, grid.in_blk
+    near = tuple(a for a in within if a != "c")
+    (
+        _, full_query, full_key, full_value, full_output, full_inner, full_outer, vectors,
+        bias_inner, queries, keys, values, attended_flat, log_totals, branch,
+    ) = forward(
+        grid,
+        (flat, packed, w_query, w_key, w_value, w_output, w_inner, w_outer),
+        (within,) + (full,) * 7,
+        (
+            (1, None, one),
+            (3, None, two),
+            (4, None, one),
+            (0, None, near),
+            (2, None, two),
+            (5, None, one),
+            (6, inner_halves[0], two),
+            (6, inner_halves[1], one),
+            (7, outer_halves[0], two),
+            (7, outer_halves[1], one),
+        ),
+        query_ids.reshape(-1, 1),
+        segment_ids[:, None, :],
+        hidden,
+        1,
+    )
+    full_query, full_key, full_value, full_output, full_outer = (
+        g.reshape(-1, width) for g in (full_query, full_key, full_value, full_output, full_outer)
+    )
+    full_inner = full_inner.reshape(-1, hidden)
+    gain_one, shift_one, bias_outer, gain_two, shift_two = (vectors[k] for k in (3, 4, 6, 7, 8))
+
+    def by_row(blocks_in):
+        blocks_in = blocks_in.reshape(blocks, rows_local, block_size, width)
+        return blocks_in.transpose(1, 0, 2, 3).reshape(rows_local, blocks * block_size, width)
+
+    keys_whole, values_whole = by_row(keys), by_row(values)
+    queries = queries.reshape(rows_local, block_size, width)
+    log_totals = log_totals[:, :HEADS].reshape(rows_local, block_size, HEADS).transpose(0, 2, 1)
+    flat_wide = flat.astype(jnp.float32)
+    stat_sums = (
+        jnp.sum(valid * flat_wide * flat_wide),
+        jnp.sum(valid * branch * branch),
+        jnp.sum(valid),
+    )
+    first, first_back = jax.vjp(
+        layer_norm, flat_wide + branch, gain_one.astype(jnp.float32), shift_one.astype(jnp.float32)
+    )
+    first_low = first.astype(jnp.bfloat16)
+    inner = plain_product(first_low, full_inner) + bias_inner
+    active_wide, gelu_back = jax.vjp(gelu_exact, inner)
+    active = active_wide.astype(jnp.bfloat16)
+    outer = plain_product(active, full_outer) + bias_outer
+    result, second_back = jax.vjp(
+        layer_norm, first + outer, gain_two.astype(jnp.float32), shift_two.astype(jnp.float32)
+    )
+    block_out = result.astype(jnp.bfloat16).reshape(tokens.shape)
+    upstream = cotangent.reshape(-1, width).astype(jnp.float32) * valid
+    grad_second, grad_gain_two, grad_shift_two = second_back(upstream)
+    grad_outer = grad_second.astype(jnp.bfloat16)
+    grad_bias_outer = jnp.sum(grad_outer.astype(jnp.float32), axis=0)
+    grad_weight_outer = left_transpose(active, grad_outer)
+    grad_active = right_transpose(grad_outer, full_outer)
+    grad_inner = gelu_back(grad_active)[0].astype(jnp.bfloat16)
+    grad_bias_inner = jnp.sum(grad_inner.astype(jnp.float32), axis=0)
+    grad_weight_inner = left_transpose(first_low, grad_inner)
+    grad_first = grad_second + right_transpose(grad_inner, full_inner)
+    grad_resid, grad_gain_one, grad_shift_one = first_back(grad_first)
+    grad_branch = grad_resid.astype(jnp.bfloat16)
+    grad_bias_output = jnp.sum(grad_branch.astype(jnp.float32), axis=0)
+    grad_weight_output = left_transpose(attended_flat, grad_branch)
+    grad_attended = right_transpose(grad_branch, full_output).astype(jnp.bfloat16)
+    grad_attended = grad_attended.reshape(rows_local, block_size, width)
+    grad_queries, key_terms, value_terms = lax.map(
+        attend_back,
+        (queries, keys_whole, values_whole, query_ids, segment_ids, log_totals, grad_attended),
+    )
+
+    def by_block(terms):
+        terms = terms.astype(jnp.bfloat16).reshape(rows_local, blocks, block_size, width)
+        return terms.transpose(1, 0, 2, 3).reshape(
+            *grid.dims(within), rows_local * block_size, width
+        )
+
+    backwards = ("c",) * ("c" in within) + near
+    grad_key_flat, grad_value_flat = scatter(
+        grid,
+        (by_block(key_terms), by_block(value_terms)),
+        (within, within),
+        ((0, None, backwards), (1, None, backwards)),
+        (jnp.bfloat16, jnp.bfloat16),
+        2,
+    )
+    grad_query_flat = grad_queries.reshape(-1, width)
+    grad_tokens = (
+        grad_resid
+        + right_transpose(grad_query_flat, full_query)
+        + right_transpose(grad_key_flat, full_key)
+        + right_transpose(grad_value_flat, full_value)
+    )
+    grad_weight_query = left_transpose(flat, grad_query_flat)
+    grad_weight_key = left_transpose(flat, grad_key_flat)
+    grad_weight_value = left_transpose(flat, grad_value_flat)
+    grad_bias_query = jnp.sum(grad_query_flat.astype(jnp.float32), axis=0)
+    grad_bias_value = jnp.sum(grad_value_flat.astype(jnp.float32), axis=0)
+    sums = (
+        grad_bias_query, grad_bias_value, grad_bias_output, grad_gain_one, grad_shift_one,
+        grad_bias_inner, grad_bias_outer, grad_gain_two, grad_shift_two,
+    )
+    terms = jnp.concatenate(
+        [g.reshape(shards, -1) for g in sums]
+        + [jnp.broadcast_to(jnp.stack(stat_sums), (shards, 3))],
+        axis=1,
+    )
+    terms = jnp.pad(terms, ((0, 0), (0, tile * 128 - ends[-1] - 3)))
+
+    def parted(grad):
+        return grad.astype(jnp.bfloat16).reshape(
+            *grid.dims(full), grad.shape[0] // shards, grad.shape[1]
+        )
+
+    one, two = ("c", "x", "y", "z"), ("c", "y", "x", "z")
+    shares = scatter(
+        grid,
+        (
+            terms.reshape(*grid.dims(full), tile, 128),
+            *(
+                parted(g)
+                for g in (
+                    grad_weight_query, grad_weight_key, grad_weight_value, grad_weight_output,
+                    grad_weight_inner, grad_weight_outer,
+                )
+            ),
+        ),
+        (full,) * 7,
+        (
+            (5, inner_halves[0], one),
+            (5, inner_halves[1], two),
+            (6, outer_halves[0], one),
+            (6, outer_halves[1], two),
+            (4, None, one),
+            (1, None, two),
+            (2, None, one),
+            (3, None, two),
+            (0, None, one),
+        ),
+        (jnp.float32,) * 7,
+        3,
+    )
+    totals = shares[0].reshape(-1)
+    small_shares = [totals[e - n : e] for e, n in zip(ends, sizes)]
+    stat_totals = totals[ends[-1] : ends[-1] + 3]
+    rms_tokens = jnp.sqrt(stat_totals[0] / (stat_totals[2] * width))
+    rms_attention = jnp.sqrt(stat_totals[1] / (stat_totals[2] * width))
+    return (
+        block_out,
+        grad_tokens.reshape(tokens.shape),
+        *shares[1:5],
+        *small_shares[:5],
+        shares[5],
+        small_shares[5],
+        shares[6],
+        *small_shares[6:],
+        rms_tokens,
+        rms_attention,
+    )
+
+
 def solution(mesh):
     placed = (
         P("rows", "blk", None),
@@ -673,8 +1036,11 @@
         P("rows", "blk", None),
     )
     grid = Grid(mesh.shape["rows"], mesh.shape["blk"])
+    devices = mesh.shape["rows"] * mesh.shape["blk"]
+    tiled = (WIDTH // devices) % 8 == 0
+    body = local_fused if tiled else local
     return jax.shard_map(
-        functools.partial(local, grid),
+        functools.partial(body, grid),
         mesh=mesh,
         in_specs=placed,
         out_specs=(

time: 342 us -> 312 us (0.912)
  matrix products: 66.3 us -> 44.2 us
  local copies, waits for them, and re-layouts: 61 us -> 50.1 us
  Pallas kernels: 188 us -> 196 us
  other arithmetic: 19.6 us -> 15 us
    dot_general x6 -> x2, matrix products: 25.9 us -> 11.6 us  [plain_product(): return jnp.dot(left, right, preferred_element_type=jnp.float32)]
    pallas_call x1, Pallas kernels: 84.8 us -> 93 us  [forward(): pl.pallas_call(functools.partial(forward_body, grid, axes_of, chunks, ahe...]
    concatenate x2 -> x1, local copies, waits for them, and re-layouts: 6.21 us -> 0.11 us  [local_fused(): jnp.concatenate([g.reshape(shards, -1) for g in sums] + [jnp.broadcast_to...]
    dot_general x6, matrix products: 14.6 us -> 9.29 us  [right_transpose(): lax.dot_general(left, right, (((1,), (1,)), ((), ())), preferred_element_...]
    convert_element_type x9 -> x0, local copies, waits for them, and re-layouts: 4.07 us -> none  [the longest x1 1.39 us: local(): shift_two.astype(jnp.float32)]
    unnamed x107 -> x80, local copies, waits for them, and re-layouts: 9.41 us -> 5.66 us
    dynamic_slice x18 -> x14, local copies, waits for them, and re-layouts: 6.49 us -> 9.83 us  [local_fused(): lax.map(attend_back, (queries, keys_whole, values_whole, query_ids, segme...]
where the time goes in v2:
time: 312 us; the launch traced here: 311 us
  Pallas kernels  196 us (63%)
  local copies, waits for them, and re-layouts  50.1 us (16%)
  matrix products  44.2 us (14%)
  other arithmetic  15 us (5%)
  between operations  5.53 us (2%)
    pallas_call x2, Pallas kernels, scatter(): pl.pallas_call(functools.partial(scatter_body, grid, axes_of, chunks, lag...  103 us
    pallas_call x1, Pallas kernels, forward(): pl.pallas_call(functools.partial(forward_body, grid, axes_of, chunks, ahe...  93 us
    dot_general x6, matrix products, left_transpose(): lax.dot_general(left, right, (((0,), (0,)), ((), ())), preferred_element_...  14.5 us
    dot_general x2, matrix products, plain_product(): return jnp.dot(left, right, preferred_element_type=jnp.float32)  11.6 us
    dynamic_slice x14, local copies, waits for them, and re-layouts, local_fused(): lax.map(attend_back, (queries, keys_whole, values_whole, query_ids, segme...  9.83 us
    dot_general x6, matrix products, right_transpose(): lax.dot_general(left, right, (((1,), (1,)), ((), ())), preferred_element_...  9.29 us
    reshape x4, local copies, waits for them, and re-layouts, by_block(): terms.astype(jnp.bfloat16).reshape(rows_local, blocks, block_size, width)  7.61 us

profile of v2, /device:TPU:0, one launch (start us, length us, event | category | flops | bytes accessed | tf_op | source)
XLA Modules:
  0.0 311.1 jit_solution(8847344478447724223)
XLA Ops:
  0.7 1.3 fusion.17
  1.9 0.8 copy.46.refs_8_
  6.8 1.3 broadcast_in_dim.51.refs_9_
  8.1 93.0 %forward.1 = (f32[4,2,2,2,16,128]{5,4,3,2,1,0:T(8,128)}, bf16[4,2,2,2,24,768]{5,4,3,2,1,0:T(8,128)(2,1)}, bf16[4,2,2,2,24,768]{5,4,3,2,1,0:T(8,128)(2,1)}, bf16[...) custom-call(bf16[256,768]{1,0:T(8,128)(2,1)} %bitcast.197, ...), custom_call_target="tpu_custom_call" | custom-call | tf_op jit(solution)/shard_map/forward/pallas_call | solution.py:566
  101.1 1.4 fusion.24
  102.7 1.0 slice_reduce_fusion.1
  103.7 10.0 %multiply_convert_fusion.1 = (bf16[256,3072]{1,0:T(8,128)(2,1)S(1)}, f32[256,3072]{1,0:T(8,128)S(1)}, f32[256,3072]{1,0:T(8,128)S(1)}) fusion(f32[3072]{0:T(1024)} %bitcast.233, bf16[768,3072]{1,0:T(8,128)(2,1)} %bitcast.225, f32[256,768]{1,0:T(8,128)S(1)} %get-tuple-element.199, f32[768]{0:T(1024)S(1)} %get-tuple-element.157, ...), kind=kOutput, calls=%fused_computation.27 | convolution fusion | flops 1260847104 | bytes 13389824 | tf_op jit(solution)/shard_map/dot_general | solution.py:387
  113.8 1.5 fusion.27
  116.1 1.1 multiply_reduce_fusion.2
  117.2 1.2 fusion.22
  118.4 0.7 convert_reduce_fusion.1
  119.2 3.6 %convolution_convert_fusion = bf16[3072,768]{1,0:T(8,128)(2,1)} fusion(bf16[256,3072]{1,0:T(8,128)(2,1)S(1)} %get-tuple-element.196, bf16[256,768]{1,0:T(8,128)(2,1)S(1)} %get-tuple-element.187), kind=kOutput, calls=%fused_computation.20 | convolution fusion | flops 1210318848 | bytes 6684672 | tf_op jit(solution)/shard_map/dot_general | solution.py:391
  122.8 2.8 convert_reduce_fusion
  125.6 3.7 %convolution_convert_fusion.1 = bf16[768,3072]{1,0:T(8,128)(2,1)} fusion(bf16[256,3072]{1,0:T(8,128)(2,1)S(1)} %get-tuple-element.189, f32[256,768]{1,0:T(8,128)S(1)} %get-tuple-element.199, f32[768]{0:T(1024)S(1)} %get-tuple-element.157, f32[768]{0:T(1024)S(1)} %get-tuple-element.158, f32[256]{0:T(256)S(1)} %fusion.15, f32[256]{0:T(256)S(1)} %broadcast_multiply_fusion.1), kind=kOutput, calls=%fused_computation.21 | convolution fusion | flops 1211301888 | bytes 7086080 | tf_op jit(solution)/shard_map/dot_general | solution.py:391
  129.3 2.3 multiply_reduce_fusion.3
  131.9 0.9 copy-done.3
  133.5 1.6 convolution_convert_fusion.2
  135.6 2.8 copy.47
  138.4 2.0 reshape.312
  140.4 1.0 copy.49
  141.4 2.0 reshape.318
  143.5 28.9 %while.14 = (s32[]{:T(128)}, bf16[2,128,768]{1,2,0:T(8,128)(2,1)}, bf16[2,512,768]{1,2,0:T(8,128)(2,1)}, bf16[2,512,768]{1,2,0:T(8,128)(2,1)}, bf16[2,512,768]{1...) while((s32[]{:T(128)}, bf16[2,128,768]{1,2,0:T(8,128)(2,1)}, ...), condition=%wide.region_10.11_spmd, body=%wide.region_8.10_spmd.sunk | while | flops 511441408 | bytes 79402960 | solution.py:922
  144.0 1.3 constant_dynamic-slice_fusion.15
  147.3 0.7 broadcast_compare_fusion.2
  148.1 1.0 constant_dynamic-slice_fusion.13
  149.7 1.1 copy.65
  150.8 2.4 multiply_reduce_fusion.9
  158.3 1.3 constant_dynamic-slice_fusion.15
  161.6 0.7 broadcast_compare_fusion.2
  162.4 1.0 constant_dynamic-slice_fusion.13
  164.0 1.1 copy.65
  165.1 2.4 multiply_reduce_fusion.9
  172.4 2.5 reshape.321
  174.9 2.4 copy.53
  177.8 2.3 copy.54
  180.2 23.6 %scatter_2.1 = (bf16[256,768]{1,0:T(8,128)(2,1)}, bf16[256,768]{1,0:T(8,128)(2,1)}) custom-call(bf16[2,2,256,768]{3,2,1,0:T(8,128)(2,1)} %bitcast.200, bf16[2,2,256,768]{3,2,1,0:T(8,128)(2,1)} %bitcast.201), custom_call_target="tpu_custom_call" | custom-call | tf_op jit(solution)/shard_map/scatter_2/pallas_call | solution.py:354
  203.7 1.1 convert_reduce_fusion.3
  205.7 1.0 fusion.11
  206.8 2.0 pad_maximum_fusion
  209.8 2.5 convolution_convert_fusion.4
  212.3 1.6 convolution_convert_fusion.3
  213.9 1.6 bitcast_convert_fusion
  215.4 79.0 %scatter_3.1 = (f32[8,128]{1,0:T(8,128)}, f32[24,768]{1,0:T(8,128)}, f32[24,768]{1,0:T(8,128)}, f32[24,768]{1,0:T(8,128)}, f32[24,768]{1,0:T(8,128)}, /*index=5*/f32[24,3072]{1,0:T(8,128)}, f32[96,768]{1,0:T(8,128)}) custom-call(f32[4,2,2,2,8,128]{5,4,3,2,1,0:T(8,128)} %bitcast.216, bf16[4,2,2,2,24,768]{5,4,3,2,1,0:T(8,128)(2,1)} %bitcast.206, ...), custom_call_target="tpu_custom_call" | custom-call | tf_op jit(solution)/shard_map/scatter_3/pallas_call | solution.py:354
  294.5 1.4 fusion.25
  297.9 1.6 fusion.26
  299.5 1.3 slice.70
  301.0 1.9 convolution_add_fusion.3
  303.5 1.4 convolution_add_fusion.1
  (191 shorter events, 28.9 us)
Async XLA Ops:
  1.9 113.7 %copy-start.37 = (s32[2,128]{1,0:T(2,128)}, s32[2,128]{1,0:T(2,128)S(1)}, u32[]{:S(2)}) copy-start(s32[2,128]{1,0:T(2,128)S(1)} %get-tuple-element.310) | copy-start | bytes 3076
  102.5 11.3 %slice-start.2 = ((s8[4718592]{0:T(1024)(128)(4,1)}), s8[4194304]{0:T(1024)(128)(4,1)S(1)}, s32[]{:S(2)}) async-start(s8[4718592]{0:T(1024)(128)(4,1)} %bitcast.229), calls=%async_computation.2 | async-start | bytes 8388608
  103.7 10.1 %slice-start.3 = ((s8[4718592]{0:T(1024)(128)(4,1)}), s8[524288]{0:T(1024)(128)(4,1)S(1)}, s32[]{:S(2)}) async-start(s8[4718592]{0:T(1024)(128)(4,1)} %bitcast.229), calls=%async_computation.3 | async-start | bytes 1048576
  113.8 2.3 copy-start.11
  113.8 2.3 copy-start.13
  119.2 10.1 %slice-start = ((s8[4718592]{0:T(1024)(128)(4,1)}), s8[4194304]{0:T(1024)(128)(4,1)S(1)}, s32[]{:S(2)}) async-start(s8[4718592]{0:T(1024)(128)(4,1)} %bitcast.226), calls=%async_computation | async-start | bytes 8388608
  122.8 6.5 %slice-start.1 = ((s8[4718592]{0:T(1024)(128)(4,1)}), s8[524288]{0:T(1024)(128)(4,1)S(1)}, s32[]{:S(2)}) async-start(s8[4718592]{0:T(1024)(128)(4,1)} %bitcast.226), calls=%async_computation.1 | async-start | bytes 1048576
  131.5 2.0 copy-start.25
  131.5 3.6 %copy-start.24 = (bf16[4,2,2,2,24,768]{5,4,3,2,1,0:T(8,128)(2,1)S(1)}, bf16[4,2,2,2,24,768]{5,4,3,2,1,0:T(8,128)(2,1)}, u32[]{:S(2)}) copy-start(bf16[4,2,2,2,24,768]{5,4,3,2,1,0:T(8,128)(2,1)} %get-tuple-element.109) | copy-start | bytes 3538948
  131.9 3.2 %copy-start.38 = (f32[256]{0:T(256)}, f32[256]{0:T(256)S(1)}, u32[]{:S(2)}) copy-start(f32[256]{0:T(256)S(1)} %negate_multiply_fusion.1) | copy-start | bytes 3076
  135.6 4.8 %copy-start.15 = (bf16[4,256,768]{2,1,0:T(8,128)(2,1)S(1)}, bf16[4,256,768]{2,1,0:T(8,128)(2,1)}, u32[]{:S(2)}) copy-start(bf16[4,256,768]{2,1,0:T(8,128)(2,1)} %get-tuple-element.110) | copy-start | bytes 4718596
  141.4 2.0 copy-start.28
  144.0 4.1 %copy-start.1 = (bf16[2,512,768]{1,2,0:T(8,128)(2,1)S(1)}, bf16[2,512,768]{1,2,0:T(8,128)(2,1)}, u32[]{:S(2)}) copy-start(bf16[2,512,768]{1,2,0:T(8,128)(2,1)} %get-tuple-element.333) | copy-start | bytes 4718596 | tf_op jit(solution)/shard_map/while
  145.3 3.7 %copy-start.14 = (bf16[2,128,768]{2,1,0:T(8,128)(2,1)S(1)}, bf16[2,128,768]{2,1,0:T(8,128)(2,1)}, u32[]{:S(2)}) copy-start(bf16[2,128,768]{2,1,0:T(8,128)(2,1)} %get-tuple-element.336) | copy-start | bytes 1179652 | tf_op jit(solution)/shard_map/while
  153.6 1.9 copy-start.18
  154.0 1.8 copy-start
  154.4 2.9 copy-start.8
  154.4 3.7 %copy-start.6 = (bf16[2,128,768]{2,1,0:T(8,128)(2,1)S(1)}, bf16[2,128,768]{2,1,0:T(8,128)(2,1)}, u32[]{:S(2)}) copy-start(bf16[2,128,768]{2,1,0:T(8,128)(2,1)} %copy-done.5) | copy-start | bytes 1179652 | tf_op jit(solution)/shard_map/while
  155.7 1.7 copy-start.19
  158.3 4.1 %copy-start.1 = (bf16[2,512,768]{1,2,0:T(8,128)(2,1)S(1)}, bf16[2,512,768]{1,2,0:T(8,128)(2,1)}, u32[]{:S(2)}) copy-start(bf16[2,512,768]{1,2,0:T(8,128)(2,1)} %get-tuple-element.333) | copy-start | bytes 4718596 | tf_op jit(solution)/shard_map/while
  159.6 3.7 %copy-start.14 = (bf16[2,128,768]{2,1,0:T(8,128)(2,1)S(1)}, bf16[2,128,768]{2,1,0:T(8,128)(2,1)}, u32[]{:S(2)}) copy-start(bf16[2,128,768]{2,1,0:T(8,128)(2,1)} %get-tuple-element.336) | copy-start | bytes 1179652 | tf_op jit(solution)/shard_map/while
  167.9 1.9 copy-start.18
  168.3 1.8 copy-start
  168.7 2.9 copy-start.8
  168.7 3.7 %copy-start.6 = (bf16[2,128,768]{2,1,0:T(8,128)(2,1)S(1)}, bf16[2,128,768]{2,1,0:T(8,128)(2,1)}, u32[]{:S(2)}) copy-start(bf16[2,128,768]{2,1,0:T(8,128)(2,1)} %copy-done.5) | copy-start | bytes 1179652 | tf_op jit(solution)/shard_map/while
  172.4 4.9 %copy-start.20 = (bf16[2,512,768]{1,2,0:T(8,128)(2,1)S(1)}, bf16[2,512,768]{1,2,0:T(8,128)(2,1)}, u32[]{:S(2)}) copy-start(bf16[2,512,768]{1,2,0:T(8,128)(2,1)} %get-tuple-element.114) | copy-start | bytes 4718596
  177.7 27.2 %copy-start.10 = (bf16[2,128,768]{1,2,0:T(8,128)(2,1)S(1)}, bf16[2,128,768]{1,2,0:T(8,128)(2,1)}, u32[]{:S(2)}) copy-start(bf16[2,128,768]{1,2,0:T(8,128)(2,1)} %get-tuple-element.111) | copy-start | bytes 1179652
  177.8 27.5 %copy-start.35 = (f32[768]{0:T(1024)S(1)}, f32[768]{0:T(1024)}, u32[]{:S(2)}) copy-start(f32[768]{0:T(1024)} %get-tuple-element.190) | copy-start | bytes 9220
  177.8 27.6 %copy-start.42 = (f32[768]{0:T(1024)S(1)}, f32[768]{0:T(1024)}, u32[]{:S(2)}) copy-start(f32[768]{0:T(1024)} %get-tuple-element.149) | copy-start | bytes 9220
  177.8 27.6 %copy-start.41 = (f32[768]{0:T(1024)S(1)}, f32[768]{0:T(1024)}, u32[]{:S(2)}) copy-start(f32[768]{0:T(1024)} %get-tuple-element.153) | copy-start | bytes 9220
  177.8 27.7 %copy-start.36 = (f32[3072]{0:T(1024)S(1)}, f32[3072]{0:T(1024)}, u32[]{:S(2)}) copy-start(f32[3072]{0:T(1024)} %get-tuple-element.188) | copy-start | bytes 36868
  177.8 27.8 %copy-start.34 = (f32[768]{0:T(1024)S(1)}, f32[768]{0:T(1024)}, u32[]{:S(2)}) copy-start(f32[768]{0:T(1024)} %get-tuple-element.186) | copy-start | bytes 9220
  177.8 27.9 %copy-start.2 = (bf16[2,128,768]{2,1,0:T(8,128)(2,1)S(1)}, bf16[2,128,768]{2,1,0:T(8,128)(2,1)}, u32[]{:S(2)}) copy-start(bf16[2,128,768]{2,1,0:T(8,128)(2,1)} %param.20) | copy-start | bytes 1179652
  177.8 27.9 %copy-start.12 = (bf16[2,128,768]{2,1,0:T(8,128)(2,1)S(1)}, bf16[2,128,768]{2,1,0:T(8,128)(2,1)}, u32[]{:S(2)}) copy-start(bf16[2,128,768]{2,1,0:T(8,128)(2,1)} %param.37) | copy-start | bytes 1179652
  177.8 27.9 %copy-start.40 = (f32[2,128]{1,0:T(2,128)S(1)}, f32[2,128]{1,0:T(2,128)}, u32[]{:S(2)}) copy-start(f32[2,128]{1,0:T(2,128)} %get-tuple-element.216) | copy-start | bytes 3076
  180.2 28.6 %copy-start.33 = (f32[768]{0:T(1024)S(1)}, f32[768]{0:T(1024)}, u32[]{:S(2)}) copy-start(f32[768]{0:T(1024)} %get-tuple-element.151) | copy-start | bytes 9220
  203.7 8.6 %copy-start.7 = (bf16[256,768]{1,0:T(8,128)(2,1)S(1)}, bf16[256,768]{1,0:T(8,128)(2,1)}, u32[]{:S(2)}) copy-start(bf16[256,768]{1,0:T(8,128)(2,1)} %get-tuple-element.117) | copy-start | bytes 1179652
  215.4 85.5 %copy-start.4 = (f32[256,768]{1,0:T(8,128)S(1)}, f32[256,768]{1,0:T(8,128)}, u32[]{:S(2)}) copy-start(f32[256,768]{1,0:T(8,128)} %copy-done.3) | copy-start | bytes 2359300
  215.4 85.5 %copy-start.39 = (f32[256]{0:T(256)S(1)}, f32[256]{0:T(256)}, u32[]{:S(2)}) copy-start(f32[256]{0:T(256)} %copy-done.38) | copy-start | bytes 3076
  294.5 8.4 %copy-start.21 = (bf16[256,768]{1,0:T(8,128)(2,1)S(1)}, bf16[256,768]{1,0:T(8,128)(2,1)}, u32[]{:S(2)}) copy-start(bf16[256,768]{1,0:T(8,128)(2,1)} %get-tuple-element.115) | copy-start | bytes 1179652
  294.5 8.4 %copy-start.23 = (bf16[4,2,2,2,24,768]{5,4,3,2,1,0:T(8,128)(2,1)S(1)}, bf16[4,2,2,2,24,768]{5,4,3,2,1,0:T(8,128)(2,1)}, u32[]{:S(2)}) copy-start(bf16[4,2,2,2,24,768]{5,4,3,2,1,0:T(8,128)(2,1)} %get-tuple-element.116) | copy-start | bytes 3538948
  301.0 2.5 copy-start.22
  302.9 2.0 copy-start.32
  302.9 2.6 copy-start.31
  302.9 3.2 %copy-start.30 = (f32[24,768]{1,0:T(8,128)S(1)}, f32[24,768]{1,0:T(8,128)}, u32[]{:S(2)}) copy-start(f32[24,768]{1,0:T(8,128)} %get-tuple-element.364) | copy-start | bytes 221188
  302.9 3.8 %copy-start.29 = (f32[24,768]{1,0:T(8,128)S(1)}, f32[24,768]{1,0:T(8,128)}, u32[]{:S(2)}) copy-start(f32[24,768]{1,0:T(8,128)} %get-tuple-element.365) | copy-start | bytes 221188
  302.9 4.5 %copy-start.27 = (f32[24,3072]{1,0:T(8,128)S(1)}, f32[24,3072]{1,0:T(8,128)}, u32[]{:S(2)}) copy-start(f32[24,3072]{1,0:T(8,128)} %get-tuple-element.371) | copy-start | bytes 884740
  302.9 5.2 %copy-start.26 = (f32[96,768]{1,0:T(8,128)S(1)}, f32[96,768]{1,0:T(8,128)}, u32[]{:S(2)}) copy-start(f32[96,768]{1,0:T(8,128)} %get-tuple-element.373) | copy-start | bytes 884740
  (10 other events, 12.3 us)

commit v3 on v2

--- a/solution.py
+++ b/solution.py
@@ -228,60 +228,58 @@
     )(*arrays)
 
 
-def scatter_body(grid, axes_of, chunks, lags, n, *refs):
-    ins, outs = refs[:n], refs[n : 2 * n]
-    send_sem, recv_sem, own_sem = refs[2 * n : 2 * n + 3]
-    scratch = list(refs[2 * n + 3 :])
-    own, landed = [], []
-    for _, _, phases in chunks:
-        own.append(scratch.pop(0))
-        landed.append([scratch.pop(0) for _ in phases])
-    me = grid.here()
-    used = []
-    for _, _, phases in chunks:
-        used += [a for a in phases if a not in used]
-    grid.greet(me, used)
-    sent = []
-
-    def source(t, j, place):
-        i, cut, phases = chunks[t]
-        axis = phases[j]
-        rest = [a for a in axes_of[i] if a not in phases[:j]]
-        lead = tuple(place if a == axis else EVERY for a in rest)
+class Scatter:
+    def __init__(self, grid, me, axes_of, chunks, ins, outs, sems, own, landed):
+        self.grid, self.me, self.axes_of, self.chunks = grid, me, axes_of, chunks
+        self.ins, self.outs = ins, outs
+        self.send_sem, self.recv_sem, self.own_sem = sems
+        self.own, self.landed = own, landed
+        self.sent, self.waiting = [], []
+
+    def source(self, t, j, place):
+        i, cut, phases = self.chunks[t]
+        rest = [a for a in self.axes_of[i] if a not in phases[:j]]
+        lead = tuple(place if a == phases[j] else EVERY for a in rest)
         if j == 0:
-            return piece(ins[i], lead, cut)
-        return landed[t][j - 1].at[(0, *lead)]
-
-    def ship(t, j):
-        axis = chunks[t][2][j]
-        for k in range(1, grid.size[axis]):
-            to = grid.toward(me, axis, k)
+            return piece(self.ins[i], lead, cut)
+        return self.landed[t][j - 1].at[(0, *lead)]
+
+    def ship(self, t, j):
+        axis = self.chunks[t][2][j]
+        for k in range(1, self.grid.size[axis]):
+            to = self.grid.toward(self.me, axis, k)
             copy = pltpu.make_async_remote_copy(
-                source(t, j, to[axis]), landed[t][j].at[k - 1],
-                send_sem.at[t, j, k - 1], recv_sem.at[t, j, k - 1],
-                device_id=grid.device(to), device_id_type=MESH,
+                self.source(t, j, to[axis]), self.landed[t][j].at[k - 1],
+                self.send_sem.at[t, j, k - 1], self.recv_sem.at[t, j, k - 1],
+                device_id=self.grid.device(to), device_id_type=MESH,
             )
             copy.start()
-            sent.append(copy)
-
-    def keep(t):
-        i, cut, phases = chunks[t]
-        return pltpu.make_async_copy(source(t, 0, me[phases[0]]), own[t], own_sem.at[t])
-
-    def absorb(t, j):
-        i, cut, phases = chunks[t]
-        axis = phases[j]
+            self.sent.append(copy)
+
+    def keep(self, t):
+        mine = self.source(t, 0, self.me[self.chunks[t][2][0]])
+        return pltpu.make_async_copy(mine, self.own[t], self.own_sem.at[t])
+
+    def launch(self, ts):
+        for t in ts:
+            self.ship(t, 0)
+            self.keep(t).start()
+
+    def absorb(self, t, j):
+        grid, me, landed = self.grid, self.me, self.landed[t]
+        i, cut, phases = self.chunks[t]
+        axis, out = phases[j], self.outs[i]
         parts = grid.size[axis] - 1
         for k in range(parts):
             pltpu.make_async_remote_copy(
-                landed[t][j].at[k], landed[t][j].at[k],
-                send_sem.at[t, j, k], recv_sem.at[t, j, k],
+                landed[j].at[k], landed[j].at[k],
+                self.send_sem.at[t, j, k], self.recv_sem.at[t, j, k],
                 device_id=grid.device(grid.toward(me, axis, 1)), device_id_type=MESH,
             ).wait_recv()
         if j == 0:
-            keep(t).wait()
-        rest = [a for a in axes_of[i] if a not in phases[: j + 1]]
-        before = [a for a in axes_of[i] if a not in phases[:j]]
+            self.keep(t).wait()
+        rest = [a for a in self.axes_of[i] if a not in phases[: j + 1]]
+        before = [a for a in self.axes_of[i] if a not in phases[:j]]
         last = j == len(phases) - 1
 
         def add(f, carry):
@@ -291,27 +289,24 @@
                 index = index // grid.size[a]
             spot = tuple(place[a] for a in rest)
             if j == 0:
-                mine = own[t][spot]
+                mine = self.own[t][spot]
             else:
-                mine = landed[t][j - 1][(0, *(place[a] for a in before))]
-            terms = [landed[t][j][(k, *spot)] for k in range(parts)]
+                mine = landed[j - 1][(0, *(place[a] for a in before))]
+            terms = [landed[j][(k, *spot)] for k in range(parts)]
             if last or parts > 1:
                 total = mine.astype(jnp.float32)
                 for term in terms:
                     total = total + term.astype(jnp.float32)
             else:
                 total = mine + terms[0]
-            if last:
-                if cut is None:
-                    outs[i][...] = total.astype(outs[i].dtype)
-                else:
-                    dim, begin, size = cut
-                    if dim == 0:
-                        outs[i][begin : begin + size, :] = total.astype(outs[i].dtype)
-                    else:
-                        outs[i][:, begin : begin + size] = total.astype(outs[i].dtype)
+            if not last:
+                landed[j][(0, *spot)] = total.astype(mine.dtype)
+            elif cut is None:
+                out[...] = total.astype(out.dtype)
+            elif cut[0] == 0:
+                out[cut[1] : cut[1] + cut[2], :] = total.astype(out.dtype)
             else:
-                landed[t][j][(0, *spot)] = total.astype(mine.dtype)
+                out[:, cut[1] : cut[1] + cut[2]] = total.astype(out.dtype)
             return carry
 
         steps = math.prod(grid.dims(rest))
@@ -319,48 +314,80 @@
             add(0, 0)
         else:
             lax.fori_loop(0, steps, add, 0)
-
-    count = len(chunks)
-    for t in range(count):
-        ship(t, 0)
-        keep(t).start()
-    stages = max(len(c[2]) for c in chunks)
-    starts = [sum(lags[:j]) for j in range(stages)]
-    for s in range(count + starts[-1]):
-        for j in range(stages):
-            t = s - starts[j]
-            if 0 <= t < count and j < len(chunks[t][2]):
-                absorb(t, j)
-                if j + 1 < len(chunks[t][2]):
-                    ship(t, j + 1)
-    for copy in sent:
-        copy.wait_send()
-
-
-def scatter(grid, arrays, axes_of, chunks, kinds, ident, lags=(1, 2, 2)):
-    count = len(chunks)
-    widest = max(grid.size.values())
+        if not last:
+            self.ship(t, j + 1)
+
+    def queue(self, ts, lags):
+        stages = max(len(self.chunks[t][2]) for t in ts)
+        starts = [sum(lags[:j]) for j in range(stages)]
+        for s in range(len(ts) + starts[-1]):
+            for j in range(stages):
+                if 0 <= s - starts[j] < len(ts) and j < len(self.chunks[ts[s - starts[j]]][2]):
+                    self.waiting.append((ts[s - starts[j]], j))
+
+    def advance(self, steps):
+        while self.waiting and steps > 0:
+            self.absorb(*self.waiting.pop(0))
+            steps -= 1
+
+    def finish(self):
+        self.advance(len(self.waiting))
+        for copy in self.sent:
+            copy.wait_send()
+
+
+def scatter_sems(grid, chunks):
+    count, widest = len(chunks), max(grid.size.values())
     stages = max(len(c[2]) for c in chunks)
     dma = pltpu.SemaphoreType.DMA
-    blocks = [a.shape[len(axes) :] for a, axes in zip(arrays, axes_of)]
+    return [dma((count, stages, widest - 1)), dma((count, stages, widest - 1)), dma((count,))]
+
+
+def scatter_room(grid, blocks, types, axes_of, chunks):
     room = []
     for i, cut, phases in chunks:
         shape = cut_shape(blocks[i], cut)
         for j in range(len(phases)):
             rest = grid.dims([a for a in axes_of[i] if a not in phases[: j + 1]])
             if j == 0:
-                room.append(pltpu.VMEM((*rest, *shape), arrays[i].dtype))
-            room.append(pltpu.VMEM((grid.size[phases[j]] - 1, *rest, *shape), arrays[i].dtype))
+                room.append(pltpu.VMEM((*rest, *shape), types[i]))
+            room.append(pltpu.VMEM((grid.size[phases[j]] - 1, *rest, *shape), types[i]))
+    return room
+
+
+def taken_apart(chunks, scratch):
+    own, landed, scratch = [], [], list(scratch)
+    for _, _, phases in chunks:
+        own.append(scratch.pop(0))
+        landed.append([scratch.pop(0) for _ in phases])
+    return own, landed
+
+
+def scatter_body(grid, axes_of, chunks, lags, n, *refs):
+    me = grid.here()
+    used = []
+    for _, _, phases in chunks:
+        used += [a for a in phases if a not in used]
+    grid.greet(me, used)
+    run = Scatter(
+        grid, me, axes_of, chunks, refs[:n], refs[n : 2 * n], refs[2 * n : 2 * n + 3],
+        *taken_apart(chunks, refs[2 * n + 3 :]),
+    )
+    run.launch(range(len(chunks)))
+    run.queue(range(len(chunks)), lags)
+    run.finish()
+
+
+def scatter(grid, arrays, axes_of, chunks, kinds, ident, lags=(1, 2, 2)):
+    blocks = [a.shape[len(axes) :] for a, axes in zip(arrays, axes_of)]
+    types = [a.dtype for a in arrays]
     return pl.pallas_call(
         functools.partial(scatter_body, grid, axes_of, chunks, lags, len(arrays)),
         out_shape=[jax.ShapeDtypeStruct(b, k) for b, k in zip(blocks, kinds)],
         in_specs=[pl.BlockSpec(memory_space=pl.ANY)] * len(arrays),
         out_specs=[pl.BlockSpec(memory_space=pltpu.VMEM)] * len(arrays),
         scratch_shapes=[
-            dma((count, stages, widest - 1)),
-            dma((count, stages, widest - 1)),
-            dma((count,)),
-            *room,
+            *scatter_sems(grid, chunks), *scatter_room(grid, blocks, types, axes_of, chunks)
         ],
         compiler_params=pltpu.CompilerParams(
             collective_id=ident, has_side_effects=True, vmem_limit_bytes=60 * 2**20
@@ -586,6 +613,211 @@
         ),
         name="forward",
     )(*arrays, column_ids, row_ids)
+
+
+def backward_body(grid, axes_of, chunks, groups, counts, *refs):
+    refs = list(refs)
+
+    def take(n):
+        found = refs[:n]
+        del refs[:n]
+        return found
+
+    grads = take(3)
+    (
+        sums_in, queries, keys, values, log_totals, grad_attended, tokens, grad_resid, w_query,
+        w_key, w_value, column_ids, row_ids,
+    ) = take(13)
+    shares = take(6)
+    grad_tokens, sums_out = take(2)
+    made = take(3)
+    terms = take(2)
+    totals = take(2)
+    grad_queries, sums = take(2)
+    sems, sum_send, sum_recv = take(3), *take(2)
+    sum_landed = take(len(grid.order))
+    me = grid.here()
+    grid.greet(me, grid.order)
+    run = Scatter(
+        grid, me, axes_of, chunks, (*grads, *made, *terms), (*shares, *totals), sems,
+        *taken_apart(chunks, refs),
+    )
+    early, between, late_query, late = groups
+    run.launch(early)
+    run.queue(early, (1, 2, 2))
+    blocks, block_rows, width = keys.shape
+    rows_local = row_ids.shape[0]
+    block = block_rows // rows_local
+    scale = HD ** (-0.5)
+    within = grid.dims(grid.in_blk)
+    sizes = [math.prod(within[k + 1 :]) for k in range(len(within))]
+
+    def places(b):
+        return tuple((b // z) % w for z, w in zip(sizes, within))
+
+    def attend_row_back(r, first, end):
+        mine = slice(r * block, (r + 1) * block)
+        same = column_ids[mine, :] == row_ids[r]
+        lane = lax.broadcasted_iota(jnp.int32, (block, 128), 1)
+        lse = log_totals[mine, :]
+
+        def pair(p, carry):
+            lanes = pl.ds(pl.multiple_of(p * 128, 128), 128)
+            query_pair = halves_apart(queries[mine, lanes])
+            grad_pair = halves_apart(grad_attended[mine, lanes])
+            key_pair = keys[:, mine, lanes].reshape(blocks * block, 128)
+            value_pair = values[:, mine, lanes].reshape(blocks * block, 128)
+            logits = masked_pair(query_pair, key_pair, same)
+            picked = [
+                jnp.sum(jnp.where(lane == 2 * p + h, lse, 0.0), axis=1, keepdims=True)
+                for h in (0, 1)
+            ]
+            probs = jnp.exp(logits - jnp.concatenate(picked, axis=0))
+            grad_probs = right_transpose(grad_pair, value_pair)
+            weighted = jnp.sum(probs * grad_probs, axis=-1, keepdims=True)
+            grad_scores = (probs * (grad_probs - weighted)).astype(jnp.bfloat16)
+            grad_query = halves_joined(plain_product(grad_scores, key_pair)) * scale
+            grad_queries[mine, lanes] = grad_query.astype(jnp.bfloat16)
+            grad_key = (left_transpose(grad_scores, query_pair) * scale).astype(jnp.bfloat16)
+            grad_value = left_transpose(probs.astype(jnp.bfloat16), grad_pair)
+            grad_value = grad_value.astype(jnp.bfloat16)
+            for b in range(blocks):
+                terms[0][(*places(b), mine, lanes)] = grad_key[b * block : (b + 1) * block]
+                terms[1][(*places(b), mine, lanes)] = grad_value[b * block : (b + 1) * block]
+            return carry
+
+        lax.fori_loop(first, end, pair, 0)
+
+    half = HEADS // 4
+    for r in range(rows_local):
+        attend_row_back(r, 0, half)
+        run.advance(counts[0])
+        attend_row_back(r, half, 2 * half)
+        run.launch(between[r])
+        run.advance(counts[1])
+
+    def weight_grad(k, right):
+        left = tokens[...]
+        wide = left_transpose(left, right).astype(jnp.bfloat16)
+        made[k][...] = wide.reshape(made[k].shape)
+
+    sums[0] = sums_in[...]
+    weight_grad(0, grad_queries[...])
+    sums[0, 0:1, :] = jnp.sum(grad_queries[...].astype(jnp.float32), axis=0, keepdims=True)
+    run.launch(late_query)
+    for r in range(rows_local):
+        for t in between[r]:
+            run.absorb(t, 0)
+    grad_tokens[...] = grad_resid[...] + right_transpose(grad_queries[...], w_query[...])
+    run.advance(counts[2])
+    for j in range(1, len(chunks[between[0][0]][2])):
+        for r in range(rows_local):
+            for t in between[r]:
+                run.absorb(t, j)
+    weight_grad(1, totals[0][...])
+    run.launch(late[:1])
+    weight_grad(2, totals[1][...])
+    run.launch(late[1:])
+    sums[0, 1:2, :] = jnp.sum(totals[1][...].astype(jnp.float32), axis=0, keepdims=True)
+    run.queue((*late_query, *late), (1, 1, 1))
+    sum_sent = []
+
+    def share_sums(j):
+        axis = grid.order[j]
+        for k in range(1, grid.size[axis]):
+            copy = pltpu.make_async_remote_copy(
+                sums.at[j], sum_landed[j].at[k - 1], sum_send.at[j, k - 1],
+                sum_recv.at[j, k - 1], device_id=grid.device(grid.toward(me, axis, k)),
+                device_id_type=MESH,
+            )
+            copy.start()
+            sum_sent.append(copy)
+
+    def add_sums(j):
+        total = sums[j]
+        for copy in sum_sent[len(sum_sent) - grid.size[grid.order[j]] + 1 :]:
+            copy.wait_recv()
+        for k in range(grid.size[grid.order[j]] - 1):
+            total = total + sum_landed[j][k]
+        return total
+
+    run.advance(counts[3])
+    share_sums(0)
+    grad_tokens[...] += right_transpose(totals[0][...], w_key[...])
+    for j in range(len(grid.order)):
+        run.advance(counts[4])
+        total = add_sums(j)
+        if j + 1 < len(grid.order):
+            sums[j + 1] = total
+            share_sums(j + 1)
+        else:
+            sums_out[...] = total
+        if j == 0:
+            grad_tokens[...] += right_transpose(totals[1][...], w_value[...])
+    run.finish()
+    for copy in sum_sent:
+        copy.wait_send()
+
+
+def backward(grid, grads, rest, ident, counts=(3, 3, 2, 2, 3)):
+    full, within = grid.order, grid.in_blk
+    low, wide = jnp.bfloat16, jnp.float32
+    queries, keys = rest[1], rest[2]
+    block_rows, width = queries.shape
+    rows_local = rest[-1].shape[0]
+    block = block_rows // rows_local
+    blocks = [g.shape[len(full) :] for g in grads]
+    rows = width // math.prod(grid.dims(full))
+    blocks += [(rows, width)] * 3 + [(block_rows, width)] * 2
+    axes_of = (full,) * 6 + (within,) * 2
+    inner_halves, outer_halves = halves(*blocks[0]), halves(*blocks[1])
+    one, two = ("c", "x", "y", "z"), ("c", "y", "x", "z")
+    backwards = ("c",) * ("c" in within) + tuple(a for a in within if a != "c")
+    chunks = [
+        (0, inner_halves[0], one),
+        (0, inner_halves[1], two),
+        (1, outer_halves[0], one),
+        (1, outer_halves[1], two),
+        (2, None, two),
+        (3, None, two),
+        (4, None, one),
+        (5, None, two),
+    ]
+    between = []
+    for r in range(rows_local):
+        cut = (0, r * block, block)
+        between.append((len(chunks), len(chunks) + 1))
+        chunks += [(6, cut, backwards), (7, cut, backwards)]
+    groups = ((0, 1, 2, 3, 4), tuple(between), (5,), (6, 7))
+    shape = jax.ShapeDtypeStruct
+    vmem, anywhere = pl.BlockSpec(memory_space=pltpu.VMEM), pl.BlockSpec(memory_space=pl.ANY)
+    parted = pltpu.VMEM((*grid.dims(full), rows, width), low)
+    spread = pltpu.VMEM((*grid.dims(within), block_rows, width), low)
+    dma = pltpu.SemaphoreType.DMA
+    widest = max(grid.size.values())
+    sums = rest[0].shape
+    return pl.pallas_call(
+        functools.partial(backward_body, grid, axes_of, tuple(chunks), groups, counts),
+        out_shape=[
+            *(shape(b, wide) for b in blocks[:6]), shape((block_rows, width), wide),
+            shape(sums, wide),
+        ],
+        in_specs=[anywhere] * 3 + [vmem] * len(rest),
+        out_specs=[vmem] * 8,
+        scratch_shapes=[
+            parted, parted, parted, spread, spread,
+            pltpu.VMEM((block_rows, width), low), pltpu.VMEM((block_rows, width), low),
+            pltpu.VMEM((block_rows, width), low), pltpu.VMEM((len(full), *sums), wide),
+            *scatter_sems(grid, chunks),
+            dma((len(full), widest - 1)), dma((len(full), widest - 1)),
+            *(pltpu.VMEM((grid.size[a] - 1, *sums), wide) for a in full),
+            *scatter_room(grid, blocks, [low] * 8, axes_of, chunks),
+        ],
+        compiler_params=pltpu.CompilerParams(
+            collective_id=ident, has_side_effects=True, vmem_limit_bytes=62 * 2**20
+        ),
+        name="backward",
+    )(*grads, *rest)
 
 
 def local(
@@ -878,13 +1110,6 @@
     full_inner = full_inner.reshape(-1, hidden)
     gain_one, shift_one, bias_outer, gain_two, shift_two = (vectors[k] for k in (3, 4, 6, 7, 8))
 
-    def by_row(blocks_in):
-        blocks_in = blocks_in.reshape(blocks, rows_local, block_size, width)
-        return blocks_in.transpose(1, 0, 2, 3).reshape(rows_local, blocks * block_size, width)
-
-    keys_whole, values_whole = by_row(keys), by_row(values)
-    queries = queries.reshape(rows_local, block_size, width)
-    log_totals = log_totals[:, :HEADS].reshape(rows_local, block_size, HEADS).transpose(0, 2, 1)
     flat_wide = flat.astype(jnp.float32)
     stat_sums = (
         jnp.sum(valid * flat_wide * flat_wide),
@@ -918,97 +1143,54 @@
     grad_bias_output = jnp.sum(grad_branch.astype(jnp.float32), axis=0)
     grad_weight_output = left_transpose(attended_flat, grad_branch)
     grad_attended = right_transpose(grad_branch, full_output).astype(jnp.bfloat16)
-    grad_attended = grad_attended.reshape(rows_local, block_size, width)
-    grad_queries, key_terms, value_terms = lax.map(
-        attend_back,
-        (queries, keys_whole, values_whole, query_ids, segment_ids, log_totals, grad_attended),
-    )
-
-    def by_block(terms):
-        terms = terms.astype(jnp.bfloat16).reshape(rows_local, blocks, block_size, width)
-        return terms.transpose(1, 0, 2, 3).reshape(
-            *grid.dims(within), rows_local * block_size, width
-        )
-
-    backwards = ("c",) * ("c" in within) + near
-    grad_key_flat, grad_value_flat = scatter(
-        grid,
-        (by_block(key_terms), by_block(value_terms)),
-        (within, within),
-        ((0, None, backwards), (1, None, backwards)),
-        (jnp.bfloat16, jnp.bfloat16),
-        2,
-    )
-    grad_query_flat = grad_queries.reshape(-1, width)
-    grad_tokens = (
-        grad_resid
-        + right_transpose(grad_query_flat, full_query)
-        + right_transpose(grad_key_flat, full_key)
-        + right_transpose(grad_value_flat, full_value)
-    )
-    grad_weight_query = left_transpose(flat, grad_query_flat)
-    grad_weight_key = left_transpose(flat, grad_key_flat)
-    grad_weight_value = left_transpose(flat, grad_value_flat)
-    grad_bias_query = jnp.sum(grad_query_flat.astype(jnp.float32), axis=0)
-    grad_bias_value = jnp.sum(grad_value_flat.astype(jnp.float32), axis=0)
-    sums = (
-        grad_bias_query, grad_bias_value, grad_bias_output, grad_gain_one, grad_shift_one,
-        grad_bias_inner, grad_bias_outer, grad_gain_two, grad_shift_two,
-    )
-    terms = jnp.concatenate(
-        [g.reshape(shards, -1) for g in sums]
-        + [jnp.broadcast_to(jnp.stack(stat_sums), (shards, 3))],
-        axis=1,
-    )
-    terms = jnp.pad(terms, ((0, 0), (0, tile * 128 - ends[-1] - 3)))
+    stats = jnp.pad(jnp.stack(stat_sums), (0, width - 3))
 
     def parted(grad):
         return grad.astype(jnp.bfloat16).reshape(
             *grid.dims(full), grad.shape[0] // shards, grad.shape[1]
         )
 
-    one, two = ("c", "x", "y", "z"), ("c", "y", "x", "z")
-    shares = scatter(
-        grid,
-        (
-            terms.reshape(*grid.dims(full), tile, 128),
+    none = jnp.zeros((1, width), jnp.float32)
+    sums = jnp.concatenate(
+        [
+            none, none,
             *(
-                parted(g)
+                g.reshape(-1, width)
                 for g in (
-                    grad_weight_query, grad_weight_key, grad_weight_value, grad_weight_output,
-                    grad_weight_inner, grad_weight_outer,
+                    grad_bias_output, grad_gain_one, grad_shift_one, grad_bias_outer,
+                    grad_gain_two, grad_shift_two, grad_bias_inner, stats,
                 )
             ),
+        ]
+    )
+    last = sums.shape[0] - 1
+    sums = jnp.pad(sums, ((0, -sums.shape[0] % 8), (0, 0)))
+    *shares, grad_tokens, totals = backward(
+        grid,
+        (parted(grad_weight_inner), parted(grad_weight_outer), parted(grad_weight_output)),
+        (
+            sums, queries, keys, values, log_totals, grad_attended, flat, grad_resid, full_query,
+            full_key, full_value, query_ids.reshape(-1, 1), segment_ids[:, None, :],
         ),
-        (full,) * 7,
-        (
-            (5, inner_halves[0], one),
-            (5, inner_halves[1], two),
-            (6, outer_halves[0], one),
-            (6, outer_halves[1], two),
-            (4, None, one),
-            (1, None, two),
-            (2, None, one),
-            (3, None, two),
-            (0, None, one),
-        ),
-        (jnp.float32,) * 7,
-        3,
-    )
-    totals = shares[0].reshape(-1)
-    small_shares = [totals[e - n : e] for e, n in zip(ends, sizes)]
-    stat_totals = totals[ends[-1] : ends[-1] + 3]
-    rms_tokens = jnp.sqrt(stat_totals[0] / (stat_totals[2] * width))
-    rms_attention = jnp.sqrt(stat_totals[1] / (stat_totals[2] * width))
+        2,
+    )
+    index = lax.axis_index("rows") * blocks + lax.axis_index("blk")
+    own = lax.dynamic_slice_in_dim(totals[:8], index * (width // shards), width // shards, 1)
+    own_inner = lax.dynamic_slice_in_dim(
+        totals[8:last].reshape(-1), index * (hidden // shards), hidden // shards
+    )
+    rms_tokens = jnp.sqrt(totals[last, 0] / (totals[last, 2] * width))
+    rms_attention = jnp.sqrt(totals[last, 1] / (totals[last, 2] * width))
     return (
         block_out,
         grad_tokens.reshape(tokens.shape),
-        *shares[1:5],
-        *small_shares[:5],
-        shares[5],
-        small_shares[5],
-        shares[6],
-        *small_shares[6:],
+        *shares[3:6],
+        shares[2],
+        *(own[k] for k in range(5)),
+        shares[0],
+        own_inner,
+        shares[1],
+        *(own[k] for k in range(5, 8)),
         rms_tokens,
         rms_attention,
     )

time: 312 us -> 280 us (0.90)
  local copies, waits for them, and re-layouts: 50.1 us -> 22.3 us
  Pallas kernels: 196 us -> 216 us
  matrix products: 44.2 us -> 25.4 us
  other arithmetic: 15 us -> 9.89 us
    pallas_call x2 -> x1, Pallas kernels: 103 us -> 123 us  [backward(): pl.pallas_call(functools.partial(backward_body, grid, axes_of, tuple(chun...]
    reshape x16 -> x9, local copies, waits for them, and re-layouts: 12.5 us -> 0.05 us  [the longest x4 0.02 us: local_fused(): g.reshape(-1, width)]
    dynamic_slice x14 -> x2, local copies, waits for them, and re-layouts: 9.83 us -> 0.66 us  [the longest x1 0.59 us: local_fused(): lax.dynamic_slice_in_dim(totals[8:last].reshape(-1), index * (hidden // s...]
    dot_general x10 -> x0, matrix products: 8.84 us -> none  [the longest x2 4.81 us: row_logits(): jnp.einsum('qhd,khd->hqk', query_heads, key_heads, preferred_element_type...]
    while x45 -> x0, local copies, waits for them, and re-layouts: 5.85 us -> none
    dot_general x6 -> x3, matrix products: 14.5 us -> 8.83 us  [left_transpose(): lax.dot_general(left, right, (((0,), (0,)), ((), ())), preferred_element_...]
    unnamed x80 -> x29, local copies, waits for them, and re-layouts: 5.66 us -> 11 us
    dot_general x6 -> x3, matrix products: 9.29 us -> 5.09 us  [right_transpose(): lax.dot_general(left, right, (((1,), (1,)), ((), ())), preferred_element_...]
where the time goes in v3:
time: 280 us; the launch traced here: 279 us
  Pallas kernels  216 us (77%)
  matrix products  25.4 us (9%)
  local copies, waits for them, and re-layouts  22.3 us (8%)
  other arithmetic  9.89 us (4%)
  between operations  5.22 us (2%)
    pallas_call x1, Pallas kernels, backward(): pl.pallas_call(functools.partial(backward_body, grid, axes_of, tuple(chun...  123 us
    pallas_call x1, Pallas kernels, forward(): pl.pallas_call(functools.partial(forward_body, grid, axes_of, chunks, ahe...  93.1 us
    dot_general x2, matrix products, plain_product(): return jnp.dot(left, right, preferred_element_type=jnp.float32)  11.5 us
    unnamed x29, local copies, waits for them, and re-layouts  11 us
    dot_general x3, matrix products, left_transpose(): lax.dot_general(left, right, (((0,), (0,)), ((), ())), preferred_element_...  8.83 us

profile of v3, /device:TPU:0, one launch (start us, length us, event | category | flops | bytes accessed | tf_op | source)
XLA Modules:
  0.0 279.2 jit_solution(1555478538667617704)
XLA Ops:
  0.7 0.7 pad_bitcast_fusion.8
  1.3 0.7 pad_bitcast_fusion.6
  2.0 0.7 pad_bitcast_fusion.4
  2.7 0.7 pad_bitcast_fusion.2
  3.3 0.7 pad_bitcast_fusion
  4.0 0.1 stack.61
  4.1 0.6 pad_convert_fusion.refs_1_
  4.7 1.3 fusion.15
  6.0 0.8 copy.37.refs_8_.refs_14_
  6.8 1.3 broadcast_in_dim.20.refs_9_.refs_15_
  8.0 93.1 %forward.1 = (f32[4,2,2,2,16,128]{5,4,3,2,1,0:T(8,128)}, bf16[4,2,2,2,24,768]{5,4,3,2,1,0:T(8,128)(2,1)}, bf16[4,2,2,2,24,768]{5,4,3,2,1,0:T(8,128)(2,1)}, bf16[...) custom-call(bf16[256,768]{1,0:T(8,128)(2,1)} %bitcast.82, ...), custom_call_target="tpu_custom_call" | custom-call | tf_op jit(solution)/shard_map/forward/pallas_call | solution.py:593
  101.1 0.9 slice_reduce_fusion.1
  102.1 1.5 fusion.22
  103.6 0.2 multiply_reduce_fusion.6
  103.9 10.0 %multiply_convert_fusion = (bf16[256,3072]{1,0:T(8,128)(2,1)S(1)}, f32[256,3072]{1,0:T(8,128)S(1)}, f32[256,3072]{1,0:T(8,128)S(1)}) fusion(f32[3072]{0:T(1024)} %bitcast.100, bf16[768,3072]{1,0:T(8,128)(2,1)} %bitcast.92, f32[256,768]{1,0:T(8,128)S(1)} %get-tuple-element.91, f32[768]{0:T(1024)S(1)} %get-tuple-element.71, f32[768]{0:T(1024)S(1)} %get-tuple-element.72, ...), kind=kOutput, calls=%fused_computation.7 | convolution fusion | flops 1260847104 | bytes 13389824 | tf_op jit(solution)/shard_map/dot_general | solution.py:414
  113.9 1.5 fusion.24
  115.4 0.2 multiply_reduce_fusion.5
  115.7 1.1 multiply_reduce_fusion.1
  116.8 1.2 fusion.20
  118.0 0.1 convert_reduce_fusion.1
  118.1 2.1 convert_reduce_fusion
  120.2 3.7 %convolution_convert_fusion.1 = bf16[768,3072]{1,0:T(8,128)(2,1)} fusion(bf16[256,3072]{1,0:T(8,128)(2,1)S(1)} %get-tuple-element.79, f32[256,768]{1,0:T(8,128)S(1)} %get-tuple-element.91, f32[768]{0:T(1024)S(1)} %get-tuple-element.71, f32[768]{0:T(1024)S(1)} %get-tuple-element.72, f32[256]{0:T(256)S(1)} %fusion.11, f32[256]{0:T(256)S(1)} %broadcast_multiply_fusion.1), kind=kOutput, calls=%fused_computation.1 | convolution fusion | flops 1211301888 | bytes 7086080 | tf_op jit(solution)/shard_map/dot_general | solution.py:418
  123.9 3.6 %convolution_convert_fusion = bf16[3072,768]{1,0:T(8,128)(2,1)} fusion(bf16[256,3072]{1,0:T(8,128)(2,1)S(1)} %get-tuple-element.88, bf16[256,768]{1,0:T(8,128)(2,1)S(1)} %get-tuple-element.81), kind=kOutput, calls=%fused_computation | convolution fusion | flops 1210318848 | bytes 6684672 | tf_op jit(solution)/shard_map/dot_general | solution.py:418
  127.5 1.8 multiply_reduce_fusion.2
  129.3 0.0 copy-start.1
  129.3 0.3 fusion.19
  129.7 0.1 convert_reduce_fusion.2
  129.8 0.4 copy-done.5
  130.3 1.5 convolution_convert_fusion.2
  131.8 1.0 fusion.7
  132.9 2.0 select_maximum_fusion
  134.9 0.1 concatenate.7
  135.0 0.6 pad.64.refs_3_
  135.6 1.3 convolution_convert_fusion.3.refs_8_
  136.9 123.2 %backward.1 = (f32[24,3072]{1,0:T(8,128)}, f32[96,768]{1,0:T(8,128)}, f32[24,768]{1,0:T(8,128)}, f32[24,768]{1,0:T(8,128)}, f32[24,768]{1,0:T(8,128)}, /*index=5...) custom-call(bf16[4,2,2,2,24,3072]{5,4,3,2,1,0:T(8,128)(2,1)} %bitcast.81, ...), custom_call_target="tpu_custom_call" | custom-call | tf_op jit(solution)/shard_map/backward/pallas_call | solution.py:799
  260.2 0.8 slice.60
  260.9 0.1 constant_dynamic-slice_fusion
  261.0 0.5 slice_bitcast_fusion
  261.6 0.7 slice.66
  262.3 0.6 dynamic_slice.11
  262.9 1.4 fusion.23
  266.3 2.1 copy.46
  268.4 1.5 copy.47
  269.9 1.5 copy.48
  271.4 1.5 copy.49
  273.0 1.5 copy.50
  274.5 1.7 copy.51
  276.2 0.7 copy.52
  (41 shorter events, 0.2 us)
Async XLA Ops:
  102.1 11.8 %slice-start.2 = ((s8[4718592]{0:T(1024)(128)(4,1)}), s8[4194304]{0:T(1024)(128)(4,1)S(1)}, s32[]{:S(2)}) async-start(s8[4718592]{0:T(1024)(128)(4,1)} %bitcast.96), calls=%async_computation.2 | async-start | bytes 8388608
  103.9 10.0 %slice-start.3 = ((s8[4718592]{0:T(1024)(128)(4,1)}), s8[524288]{0:T(1024)(128)(4,1)S(1)}, s32[]{:S(2)}) async-start(s8[4718592]{0:T(1024)(128)(4,1)} %bitcast.96), calls=%async_computation.3 | async-start | bytes 1048576
  113.9 1.8 copy-start.2
  113.9 1.8 copy-start.3
  120.2 7.3 %slice-start = ((s8[4718592]{0:T(1024)(128)(4,1)}), s8[4194304]{0:T(1024)(128)(4,1)S(1)}, s32[]{:S(2)}) async-start(s8[4718592]{0:T(1024)(128)(4,1)} %bitcast.93), calls=%async_computation | async-start | bytes 8388608
  123.9 3.6 %slice-start.1 = ((s8[4718592]{0:T(1024)(128)(4,1)}), s8[524288]{0:T(1024)(128)(4,1)S(1)}, s32[]{:S(2)}) async-start(s8[4718592]{0:T(1024)(128)(4,1)} %bitcast.93), calls=%async_computation.1 | async-start | bytes 1048576
  129.3 1.0 copy-start.5
  129.3 2.5 copy-start.1
  129.3 6.3 %copy-start.4 = (bf16[4,2,2,2,24,768]{5,4,3,2,1,0:T(8,128)(2,1)S(1)}, bf16[4,2,2,2,24,768]{5,4,3,2,1,0:T(8,128)(2,1)}, u32[]{:S(2)}) copy-start(bf16[4,2,2,2,24,768]{5,4,3,2,1,0:T(8,128)(2,1)} %get-tuple-element.51) | copy-start | bytes 3538948
  129.8 7.1 %copy-start = (f32[256,768]{1,0:T(8,128)}, f32[256,768]{1,0:T(8,128)S(1)}, u32[]{:S(2)}) copy-start(f32[256,768]{1,0:T(8,128)S(1)} %get-tuple-element.83.refs_10_) | copy-start | bytes 2359300
  260.2 16.0 %copy-start.6 = (f32[96,768]{1,0:T(8,128)S(1)}, f32[96,768]{1,0:T(8,128)}, u32[]{:S(2)}) copy-start(f32[96,768]{1,0:T(8,128)} %get-tuple-element.150) | copy-start | bytes 884740
